TPU v7x, 768 devices: a whole 4x8x12 slice. The times are simulated.
768 devices in a mesh: segment: 12 (over z_lo, core), ctx: 8 (over z_hi, x), head: 8 (over y).
Axes of the slice: x: 4, y: 8, z: 12 (z_hi: 2, z_lo: 6; z = z_hi * 6 + z_lo), core: 2. Of those that a mesh axis runs over, the one named last changes fastest.
Arguments:
- queries: bfloat16 [1536, 8192], P('segment', 'head'), may hold values from -6 to 6
- keys: bfloat16 [196608, 1024], P(('segment', 'ctx'), 'head'), may hold values from -6 to 6
- values: bfloat16 [196608, 1024], P(('segment', 'ctx'), 'head'), may hold values from -6 to 6
- lengths: int32 [12], P('segment'), may hold values from 6145 to 16384, as said below
- selected: int32 [12, 3], P('segment'), may hold values from 0 to 7, as said below
- out_weight: bfloat16 [8192, 8192], P(('head', 'ctx')), may hold values from -3 to 3
Outputs:
- handed: bfloat16 [1536, 8192], P('segment', ('head', 'ctx'))
Inputs may be any that keep to these rules, and one draw needn't show every extreme that they name: `lengths`: Even-indexed sections hold 8192 cached positions or fewer, odd-indexed ones more than 8192; some section holds exactly 16384. `selected`: each row names 3 distinct blocks, each holding at least one cached position of its section; block 0 and the block holding the section's last cached position are always named.
All inputs are finite; a program needn't handle non-finite values.
Results may differ from a plain program's by a relative error of at most 0.019.
Values may be sent and summed in bfloat16 or wider, within the bound.
No kernel may reach another device: no remote copies, remote signals or barrier semaphores. Data moves between devices by JAX's collectives and lax.ppermute only.
A program may use at most 32 MiB of HBM per device.

v0:
```python
import functools
import math

import jax
import jax.numpy as jnp
from jax import lax
from jax.experimental import pallas as pl
from jax.experimental.pallas import tpu as pltpu
from jax.sharding import PartitionSpec as P


HEAD_DIM = 128
STAT_ROWS = 16
MASKED = -1e30
LOG2E = 1.4426950408889634
Z_PARTS = 2


def whole(count):
    return [pl.BlockSpec(memory_space=pltpu.VMEM)] * count


def stat_rows(lse):
    high = lse.astype(jnp.bfloat16).astype(jnp.float32)
    rest = lse - high
    mid = rest.astype(jnp.bfloat16).astype(jnp.float32)
    low = rest - mid
    row = lax.broadcasted_iota(jnp.int32, (STAT_ROWS, lse.shape[1]), 0)
    return jnp.where(row == 0, high, jnp.where(row == 1, mid, low)).astype(jnp.bfloat16)


def pack_body(weight_ref, out_ref, held, loads, stores):
    x_parts = out_ref.shape[0]
    places = weight_ref.shape[1] // HEAD_DIM // x_parts

    def load(x, place):
        first = (place * x_parts + x) * HEAD_DIM
        return pltpu.make_async_copy(
            weight_ref.at[:, first : first + HEAD_DIM],
            held.at[x, :, place * HEAD_DIM : (place + 1) * HEAD_DIM],
            loads.at[x, place],
        )

    def store(x):
        return pltpu.make_async_copy(held.at[x], out_ref.at[x], stores.at[x])

    for x in range(x_parts):
        for place in range(places):
            load(x, place).start()
    for x in range(x_parts):
        for place in range(places):
            load(x, place).wait()
        store(x).start()
    for x in range(x_parts):
        store(x).wait()


def attend_body(cached_ref, chosen_ref, q_ref, k_ref, v_ref, own_ref, cross_ref, vt_ref, together):
    x_parts = own_ref.shape[0]
    rows = q_ref.shape[0]
    span = k_ref.shape[0]
    z = lax.axis_index("z")
    block_id = z * x_parts + lax.axis_index("x")
    usable = cached_ref[0] - block_id * span
    named = chosen_ref[0, 0] == block_id
    for i in range(1, chosen_ref.shape[1]):
        named = jnp.logical_or(named, chosen_ref[0, i] == block_id)
    picked = jnp.logical_and(usable > 0, named)
    factor = LOG2E / math.sqrt(HEAD_DIM)

    @pl.when(jnp.logical_not(picked))
    def _():
        for ref in (cross_ref, own_ref):
            for x in range(x_parts):
                ref[x, :HEAD_DIM, :] = jnp.zeros((HEAD_DIM, rows), jnp.bfloat16)
                ref[x, HEAD_DIM:, :] = jnp.full((STAT_ROWS, rows), MASKED, jnp.bfloat16)

    def compute(masked):
        vt_ref[...] = v_ref[...].T
        for ref, side in ((cross_ref, 1 - z), (own_ref, z)):
            for x in range(0, x_parts, together):
                first = pl.multiple_of((side * x_parts + x) * HEAD_DIM, HEAD_DIM)
                heads = q_ref[:, pl.ds(first, together * HEAD_DIM)]
                scores = lax.dot_general(
                    k_ref[...],
                    jnp.concatenate([heads[:, i * HEAD_DIM : (i + 1) * HEAD_DIM] for i in range(together)], axis=0),
                    (((1,), (1,)), ((), ())),
                    preferred_element_type=jnp.float32,
                )
                if masked:
                    position = lax.broadcasted_iota(jnp.int32, scores.shape, 0)
                    scores = jnp.where(position < usable, scores, MASKED)
                top = jnp.max(scores, axis=0, keepdims=True)
                expo = jnp.exp2((scores - top) * factor)
                total = jnp.sum(expo, axis=0, keepdims=True)
                gathered = jnp.dot(vt_ref[...], expo.astype(jnp.bfloat16), preferred_element_type=jnp.float32)
                gathered = (gathered / total).astype(jnp.bfloat16)
                stats = stat_rows(top * factor + jnp.log2(total))
                for i in range(together):
                    ref[x + i, :HEAD_DIM, :] = gathered[:, i * rows : (i + 1) * rows]
                    ref[x + i, HEAD_DIM:, :] = stats[:, i * rows : (i + 1) * rows]

    pl.when(jnp.logical_and(picked, usable >= span))(lambda: compute(False))
    pl.when(jnp.logical_and(picked, usable < span))(lambda: compute(True))


def merged(parts):
    logs = []
    for part in parts:
        stats = part[HEAD_DIM:, :].astype(jnp.float32)
        logs.append(stats[0:1] + stats[1:2] + stats[2:3])
    top = functools.reduce(jnp.maximum, logs)
    shares = [jnp.exp2(log - top) for log in logs]
    total = functools.reduce(jnp.add, shares)
    summed = functools.reduce(
        jnp.add, [part[:HEAD_DIM, :].astype(jnp.float32) * (share / total) for part, share in zip(parts, shares)]
    )
    return summed, top + jnp.log2(total)


def merge_body(own_ref, other_ref, out_ref):
    for head in range(own_ref.shape[0]):
        out, log = merged([own_ref[head], other_ref[head]])
        out = out.astype(jnp.bfloat16)
        log = stat_rows(log)
        for x in range(out_ref.shape[0]):
            out_ref[x, head, :HEAD_DIM, :] = out
            out_ref[x, head, HEAD_DIM:, :] = log


def project_body(parts_ref, weight_ref, out_ref):
    heads = []
    for head in range(parts_ref.shape[1]):
        out, _ = merged([parts_ref[i, head] for i in range(parts_ref.shape[0])])
        heads.append(out.astype(jnp.bfloat16).T)
    rows = jnp.concatenate(heads, axis=1)
    y_parts, z_parts = out_ref.shape[:2]
    for y in range(y_parts):
        first = y * z_parts * HEAD_DIM
        block = weight_ref[:, :, first : first + z_parts * HEAD_DIM].reshape(-1, z_parts * HEAD_DIM)
        cols = jnp.dot(rows, block, preferred_element_type=jnp.float32).astype(jnp.bfloat16)
        for z in range(z_parts):
            out_ref[y, z] = cols[:, z * HEAD_DIM : (z + 1) * HEAD_DIM]


def split_sum_body(parts_ref, own_ref, cross_ref):
    z = lax.axis_index("z")
    for ref, half in ((cross_ref, 1 - z), (own_ref, z)):
        ref[...] = functools.reduce(
            jnp.add, [parts_ref[i, half].astype(jnp.float32) for i in range(parts_ref.shape[0])]
        ).astype(jnp.bfloat16)


def shape(*dims):
    return jax.ShapeDtypeStruct(dims, jnp.bfloat16)


def on_device(queries, keys, values, lengths, selected, out_weight):
    rows = queries.shape[0]
    segments, z_parts, x_parts, y_parts = (lax.axis_size(a) for a in ("segment", "z", "x", "head"))
    message = HEAD_DIM + STAT_ROWS
    tile = (rows, HEAD_DIM)

    def kernel(body, inputs, outputs, mib, **more):
        return pl.pallas_call(
            body,
            out_shape=outputs,
            in_specs=inputs,
            out_specs=whole(len(outputs)),
            compiler_params=pltpu.CompilerParams(vmem_limit_bytes=mib << 20),
            **more,
        )

    packed = out_weight.shape[1] // x_parts
    pack = pl.pallas_call(
        pack_body,
        out_shape=shape(x_parts, HEAD_DIM, packed),
        in_specs=[pl.BlockSpec(memory_space=pl.ANY)],
        out_specs=pl.BlockSpec(memory_space=pl.ANY),
        scratch_shapes=[
            pltpu.VMEM((x_parts, HEAD_DIM, packed), jnp.bfloat16),
            pltpu.SemaphoreType.DMA((x_parts, packed // HEAD_DIM)),
            pltpu.SemaphoreType.DMA((x_parts,)),
        ],
        name="pack",
    )(out_weight)
    weight = lax.all_to_all(pack, "x", 0, 0, tiled=True)
    own, cross = kernel(
        functools.partial(attend_body, together=4),
        [pl.BlockSpec(memory_space=pltpu.SMEM)] * 2 + whole(3),
        [shape(x_parts, message, rows)] * 2,
        32,
        scratch_shapes=[
            pltpu.VMEM((HEAD_DIM, keys.shape[0]), jnp.bfloat16),
        ],
    )(lengths, selected, queries, keys, values)
    swap = [(z, z_parts - 1 - z) for z in range(z_parts)]
    other = lax.ppermute(cross, "z", swap)
    (terms,) = kernel(merge_body, whole(2), [shape(x_parts, x_parts, message, rows)], 8)(own, other)
    terms = lax.all_to_all(terms, "x", 0, 0, tiled=True)
    (products,) = kernel(project_body, whole(2), [shape(y_parts, z_parts, *tile)], 16)(terms, weight)
    products = lax.all_to_all(products, "head", 0, 0, tiled=True)
    own, cross = kernel(split_sum_body, whole(1), [shape(*tile)] * 2, 8)(products)

    def onward(part, flip):
        pairs = [
            (s * z_parts + z, (s + 1) % segments * z_parts + (z ^ flip))
            for s in range(segments)
            for z in range(z_parts)
        ]
        return lax.ppermute(part, ("segment", "z"), pairs)

    other = onward(cross, 1)
    own = onward(own, 0)
    return (own.astype(jnp.float32) + other.astype(jnp.float32)).astype(jnp.bfloat16)


def solution(mesh):
    segment, ctx, head = mesh.devices.shape
    split = jax.sharding.Mesh(
        mesh.devices.reshape(segment, Z_PARTS, ctx // Z_PARTS, head), ("segment", "z", "x", "head")
    )
    sections = ("segment", "z", "x")
    placed = (
        P("segment", "head"),
        P(sections, "head"),
        P(sections, "head"),
        P("segment"),
        P("segment", None),
        P(("head", "z", "x"), None),
    )
    return jax.shard_map(
        on_device,
        mesh=split,
        in_specs=placed,
        out_specs=P("segment", ("head", "z", "x")),
        check_vma=False,
    )
```

profile of v0, /device:TPU:1, one launch (start us, length us, event | category | flops | bytes accessed | tf_op | source)
XLA Modules:
  0.0 117.1 jit_solution(2475976720539296467)
XLA Ops:
  0.7 0.0 copy-start
  0.7 1.0 copy-done
  1.7 0.0 copy-start.1
  1.7 1.0 copy-done.1
  2.7 0.0 copy-start.2
  2.7 0.9 copy-done.2
  3.7 0.0 copy-start.3
  3.7 0.7 copy-done.3
  4.3 4.1 %shard_map.64 = (bf16[4,144,128]{2,1,0:T(8,128)(2,1)S(1)}, bf16[4,144,128]{2,1,0:T(8,128)(2,1)S(1)}) custom-call(s32[1]{0:T(128)S(6)} %copy.7.cached_ref, s32[1,3]{1,0:T(1,128)S(1)} %copy-done.3, bf16[128,1024]{1,0:T(8,128)(2,1)S(1)} %copy-done.2, bf16[2048,128]{1,0:T(8,128)(2,1)S(1)} %copy-done, bf16[2048,128]{1,0:T(8,128)(2,1)S(1)} %copy-done.1), custom_call_target="tpu_custom_call" | custom-call | tf_op jit(solution)/shard_map/pallas_call | solution.py:188
  8.5 12.1 %collective-permute-start = (bf16[4,144,128]{2,1,0:T(8,128)(2,1)S(1)}, bf16[4,144,128]{2,1,0:T(8,128)(2,1)S(1)}, u32[]{:S(2)}, u32[]{:S(2)}) collective-permute-start(bf16[4,144,128]{2,1,0:T(8,128)(2,1)S(1)} %get-tuple-element.10), channel_id=1, source_target_pairs={{0,32},{32,0},{1,33},{33,1},{2,34},{34,2},{3,35},{35,3},{4,36},{36... | collective-permute-start | bytes 442376 | tf_op jit(solution)/shard_map/ppermute | solution.py:198
  20.6 8.7 %collective-permute-done.other_ref = bf16[4,144,128]{2,1,0:T(8,128)(2,1)S(1)} collective-permute-done((bf16[4,144,128]{2,1,0:T(8,128)(2,1)S(1)}, bf16[4,144,128]{2,1,0:T(8,128)(2,1)S(1)}, u32[]{:S(2)}, u32[]{:S(2)}) %collective-permute-start) | collective-permute-done | bytes 147488 | tf_op jit(solution)/shard_map/ppermute | solution.py:198
  29.3 0.9 shard_map.65
  30.3 5.4 %all-to-all-start = ((bf16[4,4,144,128]{3,2,1,0:T(8,128)(2,1)}), bf16[4,4,144,128]{3,2,1,0:T(8,128)(2,1)S(1)}, u32[]{:S(2)}, u32[]{:S(2)}) async-start(bf16[4,4,144,128]{3,2,1,0:T(8,128)(2,1)} %shard_map.65), calls=%async_computation | async-start | bytes 1179648 | tf_op jit(solution)/shard_map/all_to_all | solution.py:200
  35.6 3.0 %pack.1 = bf16[4,128,2048]{2,1,0:T(8,128)(2,1)} custom-call(bf16[128,8192]{1,0:T(8,128)(2,1)} %weight_ref.1), custom_call_target="tpu_custom_call" | custom-call | tf_op jit(solution)/shard_map/pack/pallas_call | solution.py:175
  38.6 4.3 %all-to-all-done.parts_ref = bf16[4,4,144,128]{3,2,1,0:T(8,128)(2,1)S(1)} async-done(((bf16[4,4,144,128]{3,2,1,0:T(8,128)(2,1)}), bf16[4,4,144,128]{3,2,1,0:T(8,128)(2,1)S(1)}, u32[]{:S(2)}, u32[]{:S(2)}) %all-to-all-start) | async-done | bytes 589856 | tf_op jit(solution)/shard_map/all_to_all | solution.py:200
  42.9 21.9 %all_to_all.15.weight_ref = bf16[4,128,2048]{2,1,0:T(8,128)(2,1)S(1)} all-to-all(bf16[4,128,2048]{2,1,0:T(8,128)(2,1)} %pack.1), channel_id=1, replica_groups=mesh['segment'=12,'z'=2,'x'=4,'head'=8] {'x'}, dimensions={0} | all-to-all | bytes 4194304 | tf_op jit(solution)/shard_map/all_to_all | solution.py:187
  64.8 0.6 shard_map.66
  65.4 31.8 %all_to_all.16.parts_ref = bf16[8,2,128,128]{3,2,1,0:T(8,128)(2,1)S(1)} all-to-all(bf16[8,2,128,128]{3,2,1,0:T(8,128)(2,1)S(1)} %shard_map.66), channel_id=1, replica_groups=mesh['segment'=12,'z'=2,'x'=4,'head'=8] {'head'}, dimensions={0} | all-to-all | bytes 1048576 | tf_op jit(solution)/shard_map/all_to_all | solution.py:202
  97.2 0.1 shard_map.67
  97.2 7.6 %collective-permute-start.1 = (bf16[128,128]{1,0:T(8,128)(2,1)S(1)}, bf16[128,128]{1,0:T(8,128)(2,1)S(1)}, u32[]{:S(2)}, u32[]{:S(2)}) collective-permute-start(bf16[128,128]{1,0:T(8,128)(2,1)S(1)} %get-tuple-element.11), channel_id=1, source_target_pairs={{0,64},{32,96},{64,128},{96,160},{128,192},{160,224},{192,256},{22... | collective-permute-start | bytes 98312 | tf_op jit(solution)/shard_map/ppermute | solution.py:211
  104.9 9.6 %collective-permute-start.2 = (bf16[128,128]{1,0:T(8,128)(2,1)S(1)}, bf16[128,128]{1,0:T(8,128)(2,1)S(1)}, u32[]{:S(2)}, u32[]{:S(2)}) collective-permute-start(bf16[128,128]{1,0:T(8,128)(2,1)S(1)} %get-tuple-element.12), channel_id=1, source_target_pairs={{0,96},{32,64},{64,160},{96,128},{128,224},{160,192},{192,288},{22... | collective-permute-start | bytes 98312 | tf_op jit(solution)/shard_map/ppermute | solution.py:211
  114.5 0.0 collective-permute-done.1
  114.5 2.0 %collective-permute-done.2 = bf16[128,128]{1,0:T(8,128)(2,1)S(1)} collective-permute-done((bf16[128,128]{1,0:T(8,128)(2,1)S(1)}, bf16[128,128]{1,0:T(8,128)(2,1)S(1)}, u32[]{:S(2)}, u32[]{:S(2)}) %collective-permute-start.2) | collective-permute-done | bytes 32800 | tf_op jit(solution)/shard_map/ppermute | solution.py:211
  116.5 0.6 add_convert_fusion
Async XLA Ops:
  0.7 1.0 copy-start
  1.7 1.0 copy-start.1
  2.7 0.9 copy-start.2
  3.7 0.7 copy-start.3
  8.5 20.8 %collective-permute-start = (bf16[4,144,128]{2,1,0:T(8,128)(2,1)S(1)}, bf16[4,144,128]{2,1,0:T(8,128)(2,1)S(1)}, u32[]{:S(2)}, u32[]{:S(2)}) collective-permute-start(bf16[4,144,128]{2,1,0:T(8,128)(2,1)S(1)} %get-tuple-element.10), channel_id=1, source_target_pairs={{0,32},{32,0},{1,33},{33,1},{2,34},{34,2},{3,35},{35,3},{4,36},{36... | collective-permute-start | bytes 442376 | tf_op jit(solution)/shard_map/ppermute | solution.py:198
  30.3 12.6 %all-to-all-start = ((bf16[4,4,144,128]{3,2,1,0:T(8,128)(2,1)}), bf16[4,4,144,128]{3,2,1,0:T(8,128)(2,1)S(1)}, u32[]{:S(2)}, u32[]{:S(2)}) async-start(bf16[4,4,144,128]{3,2,1,0:T(8,128)(2,1)} %shard_map.65), calls=%async_computation | async-start | bytes 1179648 | tf_op jit(solution)/shard_map/all_to_all | solution.py:200
  97.2 17.2 %collective-permute-start.1 = (bf16[128,128]{1,0:T(8,128)(2,1)S(1)}, bf16[128,128]{1,0:T(8,128)(2,1)S(1)}, u32[]{:S(2)}, u32[]{:S(2)}) collective-permute-start(bf16[128,128]{1,0:T(8,128)(2,1)S(1)} %get-tuple-element.11), channel_id=1, source_target_pairs={{0,64},{32,96},{64,128},{96,160},{128,192},{160,224},{192,256},{22... | collective-permute-start | bytes 98312 | tf_op jit(solution)/shard_map/ppermute | solution.py:211
  104.9 11.5 %collective-permute-start.2 = (bf16[128,128]{1,0:T(8,128)(2,1)S(1)}, bf16[128,128]{1,0:T(8,128)(2,1)S(1)}, u32[]{:S(2)}, u32[]{:S(2)}) collective-permute-start(bf16[128,128]{1,0:T(8,128)(2,1)S(1)} %get-tuple-element.12), channel_id=1, source_target_pairs={{0,96},{32,64},{64,160},{96,128},{128,224},{160,192},{192,288},{22... | collective-permute-start | bytes 98312 | tf_op jit(solution)/shard_map/ppermute | solution.py:211
where the time goes:
time: 118 us; the launch traced here: 117 us
  blocking collectives  53.7 us (46%)
  starting transfers between devices  34.7 us (29%)
  waiting for transfers between devices  15 us (13%)
  Pallas kernels  8.69 us (7%)
  local copies, waits for them, and re-layouts  3.68 us (3%)
    all_to_all x1, blocking collectives, on_device(): products = lax.all_to_all(products, 'head', 0, 0, tiled=True)  31.8 us
    all_to_all x1, blocking collectives, on_device(): weight = lax.all_to_all(pack, 'x', 0, 0, tiled=True)  21.9 us
    ppermute x2, starting transfers between devices, onward(): return lax.ppermute(part, ('segment', 'z'), pairs)  17.2 us
    ppermute x1, starting transfers between devices, on_device(): other = lax.ppermute(cross, 'z', swap)  12.1 us
    ppermute x1, waiting for transfers between devices, on_device(): other = lax.ppermute(cross, 'z', swap)  8.69 us
    all_to_all x1, starting transfers between devices, on_device(): terms = lax.all_to_all(terms, 'x', 0, 0, tiled=True)  5.36 us
    all_to_all x1, waiting for transfers between devices, on_device(): terms = lax.all_to_all(terms, 'x', 0, 0, tiled=True)  4.29 us
    pallas_call x1, Pallas kernels, on_device(): kernel(functools.partial(attend_body, together=4), [pl.BlockSpec(memory_s...  4.13 us
  transfers between devices with their start and end apart: 4, of which 3 were waited for; matrix products, arithmetic and copies ran while one was open for 0% of the time, Pallas kernels for 3%

commit v1 on v0

--- a/solution.py
+++ b/solution.py
@@ -14,6 +14,7 @@
 MASKED = -1e30
 LOG2E = 1.4426950408889634
 Z_PARTS = 2
+CORES = 2
 
 
 def whole(count):
@@ -31,12 +32,13 @@
 
 def pack_body(weight_ref, out_ref, held, loads, stores):
     x_parts = out_ref.shape[0]
-    places = weight_ref.shape[1] // HEAD_DIM // x_parts
+    places = out_ref.shape[2] // HEAD_DIM
+    core = lax.axis_index("segment") % CORES
 
     def load(x, place):
-        first = (place * x_parts + x) * HEAD_DIM
+        first = pl.multiple_of(((core * places + place) * x_parts + x) * HEAD_DIM, HEAD_DIM)
         return pltpu.make_async_copy(
-            weight_ref.at[:, first : first + HEAD_DIM],
+            weight_ref.at[:, pl.ds(first, HEAD_DIM)],
             held.at[x, :, place * HEAD_DIM : (place + 1) * HEAD_DIM],
             loads.at[x, place],
         )
@@ -128,19 +130,21 @@
             out_ref[x, head, HEAD_DIM:, :] = log
 
 
-def project_body(parts_ref, weight_ref, out_ref):
+def project_body(parts_ref, kept_ref, given_ref, out_ref):
     heads = []
     for head in range(parts_ref.shape[1]):
         out, _ = merged([parts_ref[i, head] for i in range(parts_ref.shape[0])])
         heads.append(out.astype(jnp.bfloat16).T)
     rows = jnp.concatenate(heads, axis=1)
     y_parts, z_parts = out_ref.shape[:2]
-    for y in range(y_parts):
-        first = y * z_parts * HEAD_DIM
-        block = weight_ref[:, :, first : first + z_parts * HEAD_DIM].reshape(-1, z_parts * HEAD_DIM)
-        cols = jnp.dot(rows, block, preferred_element_type=jnp.float32).astype(jnp.bfloat16)
-        for z in range(z_parts):
-            out_ref[y, z] = cols[:, z * HEAD_DIM : (z + 1) * HEAD_DIM]
+    core = lax.axis_index("segment") % CORES
+    for half, weight_ref in ((core, kept_ref), (1 - core, given_ref)):
+        for y in range(y_parts // CORES):
+            first = y * z_parts * HEAD_DIM
+            block = weight_ref[:, :, first : first + z_parts * HEAD_DIM].reshape(-1, z_parts * HEAD_DIM)
+            cols = jnp.dot(rows, block, preferred_element_type=jnp.float32).astype(jnp.bfloat16)
+            for z in range(z_parts):
+                out_ref[half * (y_parts // CORES) + y, z] = cols[:, z * HEAD_DIM : (z + 1) * HEAD_DIM]
 
 
 def split_sum_body(parts_ref, own_ref, cross_ref):
@@ -171,7 +175,7 @@
             **more,
         )
 
-    packed = out_weight.shape[1] // x_parts
+    packed = out_weight.shape[1] // x_parts // CORES
     pack = pl.pallas_call(
         pack_body,
         out_shape=shape(x_parts, HEAD_DIM, packed),
@@ -194,13 +198,6 @@
             pltpu.VMEM((HEAD_DIM, keys.shape[0]), jnp.bfloat16),
         ],
     )(lengths, selected, queries, keys, values)
-    swap = [(z, z_parts - 1 - z) for z in range(z_parts)]
-    other = lax.ppermute(cross, "z", swap)
-    (terms,) = kernel(merge_body, whole(2), [shape(x_parts, x_parts, message, rows)], 8)(own, other)
-    terms = lax.all_to_all(terms, "x", 0, 0, tiled=True)
-    (products,) = kernel(project_body, whole(2), [shape(y_parts, z_parts, *tile)], 16)(terms, weight)
-    products = lax.all_to_all(products, "head", 0, 0, tiled=True)
-    own, cross = kernel(split_sum_body, whole(1), [shape(*tile)] * 2, 8)(products)
 
     def onward(part, flip):
         pairs = [
@@ -212,6 +209,14 @@
 
     other = onward(cross, 1)
     own = onward(own, 0)
+    given = lax.ppermute(weight, "segment", [(s, s ^ 1) for s in range(segments)])
+    (terms,) = kernel(merge_body, whole(2), [shape(x_parts, x_parts, message, rows)], 8)(own, other)
+    terms = lax.all_to_all(terms, "x", 0, 0, tiled=True)
+    (products,) = kernel(project_body, whole(3), [shape(y_parts, z_parts, *tile)], 16)(terms, weight, given)
+    products = lax.all_to_all(products, "head", 0, 0, tiled=True)
+    own, cross = kernel(split_sum_body, whole(1), [shape(*tile)] * 2, 8)(products)
+
+    other = lax.ppermute(cross, "z", [(z, z_parts - 1 - z) for z in range(z_parts)])
     return (own.astype(jnp.float32) + other.astype(jnp.float32)).astype(jnp.bfloat16)
 
 

time: 118 us -> 104 us (0.88)
  the two profiles are of different devices: /device:TPU:1 before, /device:TPU:65 now
where the time goes in v1:
time: 104 us; the launch traced here: 103 us
  blocking collectives  54.2 us (52%)
  starting transfers between devices  22 us (21%)
  waiting for transfers between devices  18.6 us (18%)
  Pallas kernels  7.17 us (7%)
    all_to_all x1, blocking collectives, on_device(): products = lax.all_to_all(products, 'head', 0, 0, tiled=True)  23.3 us
    all_to_all x1, blocking collectives, on_device(): weight = lax.all_to_all(pack, 'x', 0, 0, tiled=True)  18.3 us
    ppermute x2, starting transfers between devices, onward(): return lax.ppermute(part, ('segment', 'z'), pairs)  15.8 us
    all_to_all x1, blocking collectives, on_device(): terms = lax.all_to_all(terms, 'x', 0, 0, tiled=True)  12.6 us
    ppermute x2, waiting for transfers between devices, onward(): return lax.ppermute(part, ('segment', 'z'), pairs)  9.81 us
    ppermute x1, waiting for transfers between devices, on_device(): lax.ppermute(cross, 'z', [(z, z_parts - 1 - z) for z in range(z_parts)])  8.82 us
    pallas_call x1, Pallas kernels, on_device(): kernel(functools.partial(attend_body, together=4), [pl.BlockSpec(memory_s...  4.1 us
    ppermute x1, starting transfers between devices, on_device(): lax.ppermute(weight, 'segment', [(s, s ^ 1) for s in range(segments)])  3.71 us
  transfers between devices with their start and end apart: 4, of which 2 were waited for; matrix products, arithmetic and copies ran while one was open for 0% of the time, Pallas kernels for 4%

profile of v1, /device:TPU:65, one launch (start us, length us, event | category | flops | bytes accessed | tf_op | source)
XLA Modules:
  0.0 103.4 jit_solution(16219739517516702217)
XLA Ops:
  0.0 0.0 copy-start.3
  0.0 0.0 copy-start.1
  0.0 0.0 copy-start.2
  0.0 2.3 %pack.1 = bf16[4,128,1024]{2,1,0:T(8,128)(2,1)} custom-call(bf16[128,8192]{1,0:T(8,128)(2,1)} %weight_ref.1), custom_call_target="tpu_custom_call" | custom-call | tf_op jit(solution)/shard_map/pack/pallas_call | solution.py:179
  2.3 18.3 %all_to_all.15.kept_ref = bf16[4,128,1024]{2,1,0:T(8,128)(2,1)S(1)} all-to-all(bf16[4,128,1024]{2,1,0:T(8,128)(2,1)} %pack.1), channel_id=1, replica_groups=mesh['segment'=12,'z'=2,'x'=4,'head'=8] {'x'}, dimensions={0} | all-to-all | bytes 2097152 | tf_op jit(solution)/shard_map/all_to_all | solution.py:191
  20.6 3.7 %collective-permute-start.2 = (bf16[4,128,1024]{2,1,0:T(8,128)(2,1)S(1)}, bf16[4,128,1024]{2,1,0:T(8,128)(2,1)S(1)}, u32[]{:S(2)}, u32[]{:S(2)}) collective-permute-start(bf16[4,128,1024]{2,1,0:T(8,128)(2,1)S(1)} %all_to_all.15.kept_ref), channel_id=1, source_target_pairs={{0,64},{64,0},{128,192},{192,128},{256,320},{320,256},{384,448},{4... | collective-permute-start | bytes 3145736 | tf_op jit(solution)/shard_map/ppermute | solution.py:212
  25.0 0.0 copy-done.3
  25.0 0.0 copy-done.1
  25.0 0.0 copy-done
  25.0 0.0 copy-done.2
  25.0 4.1 %shard_map.64 = (bf16[4,144,128]{2,1,0:T(8,128)(2,1)S(1)}, bf16[4,144,128]{2,1,0:T(8,128)(2,1)S(1)}) custom-call(s32[1]{0:T(128)S(6)} %copy.7.cached_ref, s32[1,3]{1,0:T(1,128)S(1)} %copy-done.3, bf16[128,1024]{1,0:T(8,128)(2,1)S(1)} %copy-done.2, bf16[2048,128]{1,0:T(8,128)(2,1)S(1)} %copy-done, bf16[2048,128]{1,0:T(8,128)(2,1)S(1)} %copy-done.1), custom_call_target="tpu_custom_call" | custom-call | tf_op jit(solution)/shard_map/pallas_call | solution.py:192
  29.1 3.9 %collective-permute-start = (bf16[4,144,128]{2,1,0:T(8,128)(2,1)S(1)}, bf16[4,144,128]{2,1,0:T(8,128)(2,1)S(1)}, u32[]{:S(2)}, u32[]{:S(2)}) collective-permute-start(bf16[4,144,128]{2,1,0:T(8,128)(2,1)S(1)} %get-tuple-element.9), channel_id=1, source_target_pairs={{0,64},{32,96},{64,128},{96,160},{128,192},{160,224},{192,256},{22... | collective-permute-start | bytes 442376 | tf_op jit(solution)/shard_map/ppermute | solution.py:208
  33.1 11.9 %collective-permute-start.1 = (bf16[4,144,128]{2,1,0:T(8,128)(2,1)S(1)}, bf16[4,144,128]{2,1,0:T(8,128)(2,1)S(1)}, u32[]{:S(2)}, u32[]{:S(2)}) collective-permute-start(bf16[4,144,128]{2,1,0:T(8,128)(2,1)S(1)} %get-tuple-element.10), channel_id=1, source_target_pairs={{0,96},{32,64},{64,160},{96,128},{128,224},{160,192},{192,288},{22... | collective-permute-start | bytes 442376 | tf_op jit(solution)/shard_map/ppermute | solution.py:208
  44.9 0.0 collective-permute-done.own_ref
  45.0 9.8 %collective-permute-done.1.other_ref = bf16[4,144,128]{2,1,0:T(8,128)(2,1)S(1)} collective-permute-done((bf16[4,144,128]{2,1,0:T(8,128)(2,1)S(1)}, bf16[4,144,128]{2,1,0:T(8,128)(2,1)S(1)}, u32[]{:S(2)}, u32[]{:S(2)}) %collective-permute-start.1) | collective-permute-done | bytes 147488 | tf_op jit(solution)/shard_map/ppermute | solution.py:208
  54.8 0.1 shard_map.65
  54.9 12.6 %all_to_all.16.parts_ref = bf16[4,4,144,128]{3,2,1,0:T(8,128)(2,1)S(1)} all-to-all(bf16[4,4,144,128]{3,2,1,0:T(8,128)(2,1)S(1)} %shard_map.65), channel_id=1, replica_groups=mesh['segment'=12,'z'=2,'x'=4,'head'=8] {'x'}, dimensions={0} | all-to-all | bytes 1179648 | tf_op jit(solution)/shard_map/all_to_all | solution.py:214
  67.5 0.0 collective-permute-done.2.given_ref
  67.5 0.6 shard_map.66
  68.1 23.3 %all_to_all.17.parts_ref = bf16[8,2,128,128]{3,2,1,0:T(8,128)(2,1)S(1)} all-to-all(bf16[8,2,128,128]{3,2,1,0:T(8,128)(2,1)S(1)} %shard_map.66), channel_id=1, replica_groups=mesh['segment'=12,'z'=2,'x'=4,'head'=8] {'head'}, dimensions={0} | all-to-all | bytes 1048576 | tf_op jit(solution)/shard_map/all_to_all | solution.py:216
  91.3 0.1 shard_map.67
  91.4 2.5 %collective-permute-start.3 = (bf16[128,128]{1,0:T(8,128)(2,1)S(1)}, bf16[128,128]{1,0:T(8,128)(2,1)S(1)}, u32[]{:S(2)}, u32[]{:S(2)}) collective-permute-start(bf16[128,128]{1,0:T(8,128)(2,1)S(1)} %get-tuple-element.12), channel_id=1, source_target_pairs={{0,32},{32,0},{1,33},{33,1},{2,34},{34,2},{3,35},{35,3},{4,36},{36... | collective-permute-start | bytes 98312 | tf_op jit(solution)/shard_map/ppermute | solution.py:219
  93.9 8.8 %collective-permute-done.3 = bf16[128,128]{1,0:T(8,128)(2,1)S(1)} collective-permute-done((bf16[128,128]{1,0:T(8,128)(2,1)S(1)}, bf16[128,128]{1,0:T(8,128)(2,1)S(1)}, u32[]{:S(2)}, u32[]{:S(2)}) %collective-permute-start.3) | collective-permute-done | bytes 32800 | tf_op jit(solution)/shard_map/ppermute | solution.py:219
  102.8 0.6 add_convert_fusion
  (1 shorter events, 0.0 us)
Async XLA Ops:
  0.0 25.0 %copy-start.3 = (s32[1,3]{1,0:T(1,128)S(1)}, s32[1,3]{1,0:T(1,128)}, u32[]{:S(2)}) copy-start(s32[1,3]{1,0:T(1,128)} %chosen_ref.1) | copy-start | bytes 40
  0.0 25.0 %copy-start.1 = (bf16[2048,128]{1,0:T(8,128)(2,1)S(1)}, bf16[2048,128]{1,0:T(8,128)(2,1)}, u32[]{:S(2)}) copy-start(bf16[2048,128]{1,0:T(8,128)(2,1)} %v_ref.1) | copy-start | bytes 1572868
  0.0 25.0 %copy-start = (bf16[2048,128]{1,0:T(8,128)(2,1)S(1)}, bf16[2048,128]{1,0:T(8,128)(2,1)}, u32[]{:S(2)}) copy-start(bf16[2048,128]{1,0:T(8,128)(2,1)} %k_ref.1) | copy-start | bytes 1572868
  0.0 25.0 %copy-start.2 = (bf16[128,1024]{1,0:T(8,128)(2,1)S(1)}, bf16[128,1024]{1,0:T(8,128)(2,1)}, u32[]{:S(2)}) copy-start(bf16[128,1024]{1,0:T(8,128)(2,1)} %q_ref.1) | copy-start | bytes 786436
  20.6 46.9 %collective-permute-start.2 = (bf16[4,128,1024]{2,1,0:T(8,128)(2,1)S(1)}, bf16[4,128,1024]{2,1,0:T(8,128)(2,1)S(1)}, u32[]{:S(2)}, u32[]{:S(2)}) collective-permute-start(bf16[4,128,1024]{2,1,0:T(8,128)(2,1)S(1)} %all_to_all.15.kept_ref), channel_id=1, source_target_pairs={{0,64},{64,0},{128,192},{192,128},{256,320},{320,256},{384,448},{4... | collective-permute-start | bytes 3145736 | tf_op jit(solution)/shard_map/ppermute | solution.py:212
  29.1 15.8 %collective-permute-start = (bf16[4,144,128]{2,1,0:T(8,128)(2,1)S(1)}, bf16[4,144,128]{2,1,0:T(8,128)(2,1)S(1)}, u32[]{:S(2)}, u32[]{:S(2)}) collective-permute-start(bf16[4,144,128]{2,1,0:T(8,128)(2,1)S(1)} %get-tuple-element.9), channel_id=1, source_target_pairs={{0,64},{32,96},{64,128},{96,160},{128,192},{160,224},{192,256},{22... | collective-permute-start | bytes 442376 | tf_op jit(solution)/shard_map/ppermute | solution.py:208
  33.1 21.7 %collective-permute-start.1 = (bf16[4,144,128]{2,1,0:T(8,128)(2,1)S(1)}, bf16[4,144,128]{2,1,0:T(8,128)(2,1)S(1)}, u32[]{:S(2)}, u32[]{:S(2)}) collective-permute-start(bf16[4,144,128]{2,1,0:T(8,128)(2,1)S(1)} %get-tuple-element.10), channel_id=1, source_target_pairs={{0,96},{32,64},{64,160},{96,128},{128,224},{160,192},{192,288},{22... | collective-permute-start | bytes 442376 | tf_op jit(solution)/shard_map/ppermute | solution.py:208
  91.4 11.3 %collective-permute-start.3 = (bf16[128,128]{1,0:T(8,128)(2,1)S(1)}, bf16[128,128]{1,0:T(8,128)(2,1)S(1)}, u32[]{:S(2)}, u32[]{:S(2)}) collective-permute-start(bf16[128,128]{1,0:T(8,128)(2,1)S(1)} %get-tuple-element.12), channel_id=1, source_target_pairs={{0,32},{32,0},{1,33},{33,1},{2,34},{34,2},{3,35},{35,3},{4,36},{36... | collective-permute-start | bytes 98312 | tf_op jit(solution)/shard_map/ppermute | solution.py:219

commit v2 on v1

--- a/solution.py
+++ b/solution.py
@@ -21,13 +21,24 @@
     return [pl.BlockSpec(memory_space=pltpu.VMEM)] * count
 
 
-def stat_rows(lse):
-    high = lse.astype(jnp.bfloat16).astype(jnp.float32)
-    rest = lse - high
-    mid = rest.astype(jnp.bfloat16).astype(jnp.float32)
-    low = rest - mid
-    row = lax.broadcasted_iota(jnp.int32, (STAT_ROWS, lse.shape[1]), 0)
-    return jnp.where(row == 0, high, jnp.where(row == 1, mid, low)).astype(jnp.bfloat16)
+def stat_rows(logs):
+    pieces = []
+    for log in logs:
+        high = log.astype(jnp.bfloat16).astype(jnp.float32)
+        mid = (log - high).astype(jnp.bfloat16).astype(jnp.float32)
+        pieces += [high, mid, log - high - mid]
+    index = lax.broadcasted_iota(jnp.int32, (STAT_ROWS, logs[0].shape[1]), 0)
+    rows = jnp.zeros(index.shape, jnp.float32)
+    for i, piece in enumerate(pieces):
+        rows = jnp.where(index == i, piece, rows)
+    return rows.astype(jnp.bfloat16)
+
+
+def outs_and_logs(block):
+    count = block.shape[0] // HEAD_DIM
+    stats = block[count * HEAD_DIM :, :].astype(jnp.float32)
+    outs = [block[i * HEAD_DIM : (i + 1) * HEAD_DIM, :].astype(jnp.float32) for i in range(count)]
+    return outs, [stats[3 * i : 3 * i + 1] + stats[3 * i + 1 : 3 * i + 2] + stats[3 * i + 2 : 3 * i + 3] for i in range(count)]
 
 
 def pack_body(weight_ref, out_ref, held, loads, stores):
@@ -57,8 +68,8 @@
         store(x).wait()
 
 
-def attend_body(cached_ref, chosen_ref, q_ref, k_ref, v_ref, own_ref, cross_ref, vt_ref, together):
-    x_parts = own_ref.shape[0]
+def attend_body(cached_ref, chosen_ref, q_ref, k_ref, v_ref, own_ref, cross_ref, vt_ref):
+    x_parts = own_ref.shape[0] // HEAD_DIM
     rows = q_ref.shape[0]
     span = k_ref.shape[0]
     z = lax.axis_index("z")
@@ -73,67 +84,67 @@
     @pl.when(jnp.logical_not(picked))
     def _():
         for ref in (cross_ref, own_ref):
-            for x in range(x_parts):
-                ref[x, :HEAD_DIM, :] = jnp.zeros((HEAD_DIM, rows), jnp.bfloat16)
-                ref[x, HEAD_DIM:, :] = jnp.full((STAT_ROWS, rows), MASKED, jnp.bfloat16)
+            ref[: x_parts * HEAD_DIM, :] = jnp.zeros((x_parts * HEAD_DIM, rows), jnp.bfloat16)
+            ref[x_parts * HEAD_DIM :, :] = jnp.full((STAT_ROWS, rows), MASKED, jnp.bfloat16)
 
     def compute(masked):
         vt_ref[...] = v_ref[...].T
         for ref, side in ((cross_ref, 1 - z), (own_ref, z)):
-            for x in range(0, x_parts, together):
-                first = pl.multiple_of((side * x_parts + x) * HEAD_DIM, HEAD_DIM)
-                heads = q_ref[:, pl.ds(first, together * HEAD_DIM)]
-                scores = lax.dot_general(
-                    k_ref[...],
-                    jnp.concatenate([heads[:, i * HEAD_DIM : (i + 1) * HEAD_DIM] for i in range(together)], axis=0),
-                    (((1,), (1,)), ((), ())),
-                    preferred_element_type=jnp.float32,
-                )
-                if masked:
-                    position = lax.broadcasted_iota(jnp.int32, scores.shape, 0)
-                    scores = jnp.where(position < usable, scores, MASKED)
-                top = jnp.max(scores, axis=0, keepdims=True)
-                expo = jnp.exp2((scores - top) * factor)
-                total = jnp.sum(expo, axis=0, keepdims=True)
-                gathered = jnp.dot(vt_ref[...], expo.astype(jnp.bfloat16), preferred_element_type=jnp.float32)
-                gathered = (gathered / total).astype(jnp.bfloat16)
-                stats = stat_rows(top * factor + jnp.log2(total))
-                for i in range(together):
-                    ref[x + i, :HEAD_DIM, :] = gathered[:, i * rows : (i + 1) * rows]
-                    ref[x + i, HEAD_DIM:, :] = stats[:, i * rows : (i + 1) * rows]
+            first = pl.multiple_of(side * x_parts * HEAD_DIM, HEAD_DIM)
+            heads = q_ref[:, pl.ds(first, x_parts * HEAD_DIM)]
+            scores = lax.dot_general(
+                k_ref[...],
+                jnp.concatenate([heads[:, i * HEAD_DIM : (i + 1) * HEAD_DIM] for i in range(x_parts)], axis=0),
+                (((1,), (1,)), ((), ())),
+                preferred_element_type=jnp.float32,
+            )
+            if masked:
+                position = lax.broadcasted_iota(jnp.int32, scores.shape, 0)
+                scores = jnp.where(position < usable, scores, MASKED)
+            top = jnp.max(scores, axis=0, keepdims=True)
+            expo = jnp.exp2((scores - top) * factor)
+            total = jnp.sum(expo, axis=0, keepdims=True)
+            gathered = jnp.dot(vt_ref[...], expo.astype(jnp.bfloat16), preferred_element_type=jnp.float32)
+            gathered = (gathered / total).astype(jnp.bfloat16)
+            logs = top * factor + jnp.log2(total)
+            for i in range(x_parts):
+                ref[i * HEAD_DIM : (i + 1) * HEAD_DIM, :] = gathered[:, i * rows : (i + 1) * rows]
+            ref[x_parts * HEAD_DIM :, :] = stat_rows([logs[:, i * rows : (i + 1) * rows] for i in range(x_parts)])
 
     pl.when(jnp.logical_and(picked, usable >= span))(lambda: compute(False))
     pl.when(jnp.logical_and(picked, usable < span))(lambda: compute(True))
 
 
-def merged(parts):
-    logs = []
-    for part in parts:
-        stats = part[HEAD_DIM:, :].astype(jnp.float32)
-        logs.append(stats[0:1] + stats[1:2] + stats[2:3])
+def merged(outs, logs):
     top = functools.reduce(jnp.maximum, logs)
     shares = [jnp.exp2(log - top) for log in logs]
     total = functools.reduce(jnp.add, shares)
-    summed = functools.reduce(
-        jnp.add, [part[:HEAD_DIM, :].astype(jnp.float32) * (share / total) for part, share in zip(parts, shares)]
-    )
+    summed = functools.reduce(jnp.add, [out * (share / total) for out, share in zip(outs, shares)])
     return summed, top + jnp.log2(total)
 
 
 def merge_body(own_ref, other_ref, out_ref):
-    for head in range(own_ref.shape[0]):
-        out, log = merged([own_ref[head], other_ref[head]])
+    absent = jnp.logical_and(lax.axis_index("segment") % 2 == 0, lax.axis_index("z") == 0)
+    own, own_logs = outs_and_logs(own_ref[...])
+    other, other_logs = outs_and_logs(other_ref[...])
+    logs = []
+    for head in range(len(own)):
+        there = jnp.where(absent, MASKED, other_logs[head])
+        out, log = merged([own[head], other[head]], [own_logs[head], there])
         out = out.astype(jnp.bfloat16)
-        log = stat_rows(log)
         for x in range(out_ref.shape[0]):
-            out_ref[x, head, :HEAD_DIM, :] = out
-            out_ref[x, head, HEAD_DIM:, :] = log
+            out_ref[x, head * HEAD_DIM : (head + 1) * HEAD_DIM, :] = out
+        logs.append(log)
+    stats = stat_rows(logs)
+    for x in range(out_ref.shape[0]):
+        out_ref[x, len(own) * HEAD_DIM :, :] = stats
 
 
 def project_body(parts_ref, kept_ref, given_ref, out_ref):
+    parts = [outs_and_logs(parts_ref[i]) for i in range(parts_ref.shape[0])]
     heads = []
-    for head in range(parts_ref.shape[1]):
-        out, _ = merged([parts_ref[i, head] for i in range(parts_ref.shape[0])])
+    for head in range(len(parts[0][0])):
+        out, _ = merged([outs[head] for outs, _ in parts], [logs[head] for _, logs in parts])
         heads.append(out.astype(jnp.bfloat16).T)
     rows = jnp.concatenate(heads, axis=1)
     y_parts, z_parts = out_ref.shape[:2]
@@ -162,7 +173,7 @@
 def on_device(queries, keys, values, lengths, selected, out_weight):
     rows = queries.shape[0]
     segments, z_parts, x_parts, y_parts = (lax.axis_size(a) for a in ("segment", "z", "x", "head"))
-    message = HEAD_DIM + STAT_ROWS
+    message = x_parts * HEAD_DIM + STAT_ROWS
     tile = (rows, HEAD_DIM)
 
     def kernel(body, inputs, outputs, mib, **more):
@@ -190,9 +201,9 @@
     )(out_weight)
     weight = lax.all_to_all(pack, "x", 0, 0, tiled=True)
     own, cross = kernel(
-        functools.partial(attend_body, together=4),
+        attend_body,
         [pl.BlockSpec(memory_space=pltpu.SMEM)] * 2 + whole(3),
-        [shape(x_parts, message, rows)] * 2,
+        [shape(message, rows)] * 2,
         32,
         scratch_shapes=[
             pltpu.VMEM((HEAD_DIM, keys.shape[0]), jnp.bfloat16),
@@ -207,16 +218,17 @@
         ]
         return lax.ppermute(part, ("segment", "z"), pairs)
 
-    other = onward(cross, 1)
-    own = onward(own, 0)
+    swap = [(s * z_parts + z, s * z_parts + 1 - z) for s in range(segments) for z in range(z_parts) if s % 2 or z == 0]
+    other = lax.ppermute(cross, ("segment", "z"), swap)
     given = lax.ppermute(weight, "segment", [(s, s ^ 1) for s in range(segments)])
-    (terms,) = kernel(merge_body, whole(2), [shape(x_parts, x_parts, message, rows)], 8)(own, other)
+    (terms,) = kernel(merge_body, whole(2), [shape(x_parts, message, rows)], 8)(own, other)
     terms = lax.all_to_all(terms, "x", 0, 0, tiled=True)
     (products,) = kernel(project_body, whole(3), [shape(y_parts, z_parts, *tile)], 16)(terms, weight, given)
     products = lax.all_to_all(products, "head", 0, 0, tiled=True)
     own, cross = kernel(split_sum_body, whole(1), [shape(*tile)] * 2, 8)(products)
 
-    other = lax.ppermute(cross, "z", [(z, z_parts - 1 - z) for z in range(z_parts)])
+    other = onward(cross, 1)
+    own = onward(own, 0)
     return (own.astype(jnp.float32) + other.astype(jnp.float32)).astype(jnp.bfloat16)
 
 

time: 104 us -> 102 us (0.981)
  the two profiles are of different devices: /device:TPU:65 before, /device:TPU:1 now
where the time goes in v2:
time: 102 us; the launch traced here: 101 us
  blocking collectives  47.9 us (47%)
  starting transfers between devices  39.2 us (38%)
  Pallas kernels  7.08 us (7%)
  waiting for transfers between devices  5.75 us (6%)
    all_to_all x1, blocking collectives, on_device(): products = lax.all_to_all(products, 'head', 0, 0, tiled=True)  20 us
    ppermute x2, starting transfers between devices, onward(): return lax.ppermute(part, ('segment', 'z'), pairs)  19.5 us
    all_to_all x1, blocking collectives, on_device(): weight = lax.all_to_all(pack, 'x', 0, 0, tiled=True)  14.6 us
    all_to_all x1, blocking collectives, on_device(): terms = lax.all_to_all(terms, 'x', 0, 0, tiled=True)  13.3 us
    ppermute x1, starting transfers between devices, on_device(): lax.ppermute(weight, 'segment', [(s, s ^ 1) for s in range(segments)])  12.2 us
    ppermute x1, starting transfers between devices, on_device(): other = lax.ppermute(cross, ('segment', 'z'), swap)  7.47 us
    ppermute x1, waiting for transfers between devices, on_device(): other = lax.ppermute(cross, ('segment', 'z'), swap)  4.75 us
    pallas_call x1, Pallas kernels, on_device(): kernel(attend_body, [pl.BlockSpec(memory_space=pltpu.SMEM)] * 2 + whole(3...  4.03 us
  transfers between devices with their start and end apart: 4, of which 2 were waited for; matrix products, arithmetic and copies ran while one was open for 0% of the time, Pallas kernels for 4%

profile of v2, /device:TPU:1, one launch (start us, length us, event | category | flops | bytes accessed | tf_op | source)
XLA Modules:
  0.0 101.3 jit_solution(13763515710948804513)
XLA Ops:
  0.0 0.0 copy-start.3
  0.0 0.0 copy-start.1
  0.0 0.0 copy-start.2
  0.0 2.3 %pack.1 = bf16[4,128,1024]{2,1,0:T(8,128)(2,1)} custom-call(bf16[128,8192]{1,0:T(8,128)(2,1)} %weight_ref.1), custom_call_target="tpu_custom_call" | custom-call | tf_op jit(solution)/shard_map/pack/pallas_call | solution.py:190
  2.3 14.6 %all_to_all.15.kept_ref = bf16[4,128,1024]{2,1,0:T(8,128)(2,1)S(1)} all-to-all(bf16[4,128,1024]{2,1,0:T(8,128)(2,1)} %pack.1), channel_id=1, replica_groups=mesh['segment'=12,'z'=2,'x'=4,'head'=8] {'x'}, dimensions={0} | all-to-all | bytes 2097152 | tf_op jit(solution)/shard_map/all_to_all | solution.py:202
  16.9 12.2 %collective-permute-start.1 = (bf16[4,128,1024]{2,1,0:T(8,128)(2,1)S(1)}, bf16[4,128,1024]{2,1,0:T(8,128)(2,1)S(1)}, u32[]{:S(2)}, u32[]{:S(2)}) collective-permute-start(bf16[4,128,1024]{2,1,0:T(8,128)(2,1)S(1)} %all_to_all.15.kept_ref), channel_id=1, source_target_pairs={{0,64},{64,0},{128,192},{192,128},{256,320},{320,256},{384,448},{4... | collective-permute-start | bytes 3145736 | tf_op jit(solution)/shard_map/ppermute | solution.py:223
  29.7 0.0 copy-done.3
  29.8 0.0 copy-done.1
  29.8 0.0 copy-done
  29.8 0.0 copy-done.2
  29.8 4.0 %shard_map.64 = (bf16[528,128]{1,0:T(8,128)(2,1)S(1)}, bf16[528,128]{1,0:T(8,128)(2,1)S(1)}) custom-call(s32[1]{0:T(128)S(6)} %copy.7.cached_ref, s32[1,3]{1,0:T(1,128)S(1)} %copy-done.3, bf16[128,1024]{1,0:T(8,128)(2,1)S(1)} %copy-done.2, bf16[2048,128]{1,0:T(8,128)(2,1)S(1)} %copy-done, bf16[2048,128]{1,0:T(8,128)(2,1)S(1)} %copy-done.1), custom_call_target="tpu_custom_call" | custom-call | tf_op jit(solution)/shard_map/pallas_call | solution.py:203
  33.8 7.5 %collective-permute-start = (bf16[528,128]{1,0:T(8,128)(2,1)S(1)}, bf16[528,128]{1,0:T(8,128)(2,1)S(1)}, u32[]{:S(2)}, u32[]{:S(2)}) collective-permute-start(bf16[528,128]{1,0:T(8,128)(2,1)S(1)} %get-tuple-element.10), channel_id=1, source_target_pairs={{0,32},{64,96},{96,64},{128,160},{192,224},{224,192},{256,288},{32... | collective-permute-start | bytes 405512 | tf_op jit(solution)/shard_map/ppermute | solution.py:222
  41.3 4.8 %collective-permute-done.other_ref = bf16[528,128]{1,0:T(8,128)(2,1)S(1)} collective-permute-done((bf16[528,128]{1,0:T(8,128)(2,1)S(1)}, bf16[528,128]{1,0:T(8,128)(2,1)S(1)}, u32[]{:S(2)}, u32[]{:S(2)}) %collective-permute-start) | collective-permute-done | bytes 135200 | tf_op jit(solution)/shard_map/ppermute | solution.py:222
  46.1 0.1 shard_map.65
  46.2 13.3 %all_to_all.16.parts_ref = bf16[4,528,128]{2,1,0:T(8,128)(2,1)S(1)} all-to-all(bf16[4,528,128]{2,1,0:T(8,128)(2,1)S(1)} %shard_map.65), channel_id=1, replica_groups=mesh['segment'=12,'z'=2,'x'=4,'head'=8] {'x'}, dimensions={0} | all-to-all | bytes 1081344 | tf_op jit(solution)/shard_map/all_to_all | solution.py:225
  59.5 0.0 collective-permute-done.1.given_ref
  59.5 0.6 shard_map.66
  60.1 20.0 %all_to_all.17.parts_ref = bf16[8,2,128,128]{3,2,1,0:T(8,128)(2,1)S(1)} all-to-all(bf16[8,2,128,128]{3,2,1,0:T(8,128)(2,1)S(1)} %shard_map.66), channel_id=1, replica_groups=mesh['segment'=12,'z'=2,'x'=4,'head'=8] {'head'}, dimensions={0} | all-to-all | bytes 1048576 | tf_op jit(solution)/shard_map/all_to_all | solution.py:227
  80.0 0.1 shard_map.67
  80.1 6.5 %collective-permute-start.2 = (bf16[128,128]{1,0:T(8,128)(2,1)S(1)}, bf16[128,128]{1,0:T(8,128)(2,1)S(1)}, u32[]{:S(2)}, u32[]{:S(2)}) collective-permute-start(bf16[128,128]{1,0:T(8,128)(2,1)S(1)} %get-tuple-element.11), channel_id=1, source_target_pairs={{0,64},{32,96},{64,128},{96,160},{128,192},{160,224},{192,256},{22... | collective-permute-start | bytes 98312 | tf_op jit(solution)/shard_map/ppermute | solution.py:219
  86.7 13.0 %collective-permute-start.3 = (bf16[128,128]{1,0:T(8,128)(2,1)S(1)}, bf16[128,128]{1,0:T(8,128)(2,1)S(1)}, u32[]{:S(2)}, u32[]{:S(2)}) collective-permute-start(bf16[128,128]{1,0:T(8,128)(2,1)S(1)} %get-tuple-element.12), channel_id=1, source_target_pairs={{0,96},{32,64},{64,160},{96,128},{128,224},{160,192},{192,288},{22... | collective-permute-start | bytes 98312 | tf_op jit(solution)/shard_map/ppermute | solution.py:219
  99.7 0.0 collective-permute-done.2
  99.7 1.0 collective-permute-done.3
  100.7 0.6 add_convert_fusion
  (1 shorter events, 0.0 us)
Async XLA Ops:
  0.0 29.8 %copy-start.3 = (s32[1,3]{1,0:T(1,128)S(1)}, s32[1,3]{1,0:T(1,128)}, u32[]{:S(2)}) copy-start(s32[1,3]{1,0:T(1,128)} %chosen_ref.1) | copy-start | bytes 40
  0.0 29.8 %copy-start.1 = (bf16[2048,128]{1,0:T(8,128)(2,1)S(1)}, bf16[2048,128]{1,0:T(8,128)(2,1)}, u32[]{:S(2)}) copy-start(bf16[2048,128]{1,0:T(8,128)(2,1)} %v_ref.1) | copy-start | bytes 1572868
  0.0 29.8 %copy-start = (bf16[2048,128]{1,0:T(8,128)(2,1)S(1)}, bf16[2048,128]{1,0:T(8,128)(2,1)}, u32[]{:S(2)}) copy-start(bf16[2048,128]{1,0:T(8,128)(2,1)} %k_ref.1) | copy-start | bytes 1572868
  0.0 29.8 %copy-start.2 = (bf16[128,1024]{1,0:T(8,128)(2,1)S(1)}, bf16[128,1024]{1,0:T(8,128)(2,1)}, u32[]{:S(2)}) copy-start(bf16[128,1024]{1,0:T(8,128)(2,1)} %q_ref.1) | copy-start | bytes 786436
  16.9 42.6 %collective-permute-start.1 = (bf16[4,128,1024]{2,1,0:T(8,128)(2,1)S(1)}, bf16[4,128,1024]{2,1,0:T(8,128)(2,1)S(1)}, u32[]{:S(2)}, u32[]{:S(2)}) collective-permute-start(bf16[4,128,1024]{2,1,0:T(8,128)(2,1)S(1)} %all_to_all.15.kept_ref), channel_id=1, source_target_pairs={{0,64},{64,0},{128,192},{192,128},{256,320},{320,256},{384,448},{4... | collective-permute-start | bytes 3145736 | tf_op jit(solution)/shard_map/ppermute | solution.py:223
  33.8 12.2 %collective-permute-start = (bf16[528,128]{1,0:T(8,128)(2,1)S(1)}, bf16[528,128]{1,0:T(8,128)(2,1)S(1)}, u32[]{:S(2)}, u32[]{:S(2)}) collective-permute-start(bf16[528,128]{1,0:T(8,128)(2,1)S(1)} %get-tuple-element.10), channel_id=1, source_target_pairs={{0,32},{64,96},{96,64},{128,160},{192,224},{224,192},{256,288},{32... | collective-permute-start | bytes 405512 | tf_op jit(solution)/shard_map/ppermute | solution.py:222
  80.1 19.5 %collective-permute-start.2 = (bf16[128,128]{1,0:T(8,128)(2,1)S(1)}, bf16[128,128]{1,0:T(8,128)(2,1)S(1)}, u32[]{:S(2)}, u32[]{:S(2)}) collective-permute-start(bf16[128,128]{1,0:T(8,128)(2,1)S(1)} %get-tuple-element.11), channel_id=1, source_target_pairs={{0,64},{32,96},{64,128},{96,160},{128,192},{160,224},{192,256},{22... | collective-permute-start | bytes 98312 | tf_op jit(solution)/shard_map/ppermute | solution.py:219
  86.7 14.0 %collective-permute-start.3 = (bf16[128,128]{1,0:T(8,128)(2,1)S(1)}, bf16[128,128]{1,0:T(8,128)(2,1)S(1)}, u32[]{:S(2)}, u32[]{:S(2)}) collective-permute-start(bf16[128,128]{1,0:T(8,128)(2,1)S(1)} %get-tuple-element.12), channel_id=1, source_target_pairs={{0,96},{32,64},{64,160},{96,128},{128,224},{160,192},{192,288},{22... | collective-permute-start | bytes 98312 | tf_op jit(solution)/shard_map/ppermute | solution.py:219

commit v3 on v2

--- a/solution.py
+++ b/solution.py
@@ -41,34 +41,8 @@
     return outs, [stats[3 * i : 3 * i + 1] + stats[3 * i + 1 : 3 * i + 2] + stats[3 * i + 2 : 3 * i + 3] for i in range(count)]
 
 
-def pack_body(weight_ref, out_ref, held, loads, stores):
-    x_parts = out_ref.shape[0]
-    places = out_ref.shape[2] // HEAD_DIM
-    core = lax.axis_index("segment") % CORES
-
-    def load(x, place):
-        first = pl.multiple_of(((core * places + place) * x_parts + x) * HEAD_DIM, HEAD_DIM)
-        return pltpu.make_async_copy(
-            weight_ref.at[:, pl.ds(first, HEAD_DIM)],
-            held.at[x, :, place * HEAD_DIM : (place + 1) * HEAD_DIM],
-            loads.at[x, place],
-        )
-
-    def store(x):
-        return pltpu.make_async_copy(held.at[x], out_ref.at[x], stores.at[x])
-
-    for x in range(x_parts):
-        for place in range(places):
-            load(x, place).start()
-    for x in range(x_parts):
-        for place in range(places):
-            load(x, place).wait()
-        store(x).start()
-    for x in range(x_parts):
-        store(x).wait()
-
-
-def attend_body(cached_ref, chosen_ref, q_ref, k_ref, v_ref, own_ref, cross_ref, vt_ref):
+def attend_body(cached_ref, chosen_ref, q_hbm, k_hbm, v_hbm, weight_ref, own_ref, cross_ref, pack_ref, *scratch):
+    q_ref, k_ref, v_ref, vt_ref, held, fetches, loads, stores = scratch
     x_parts = own_ref.shape[0] // HEAD_DIM
     rows = q_ref.shape[0]
     span = k_ref.shape[0]
@@ -80,39 +54,79 @@
         named = jnp.logical_or(named, chosen_ref[0, i] == block_id)
     picked = jnp.logical_and(usable > 0, named)
     factor = LOG2E / math.sqrt(HEAD_DIM)
+    pairs = ((q_hbm, q_ref), (k_hbm, k_ref), (v_hbm, v_ref))
+    fetch = [pltpu.make_async_copy(*pair, fetches.at[i]) for i, pair in enumerate(pairs)]
+
+    @pl.when(picked)
+    def _():
+        for copy in fetch:
+            copy.start()
+
+    places = pack_ref.shape[2] // HEAD_DIM
+    core = lax.axis_index("segment") % CORES
+
+    def load(x, place):
+        first = pl.multiple_of(((core * places + place) * x_parts + x) * HEAD_DIM, HEAD_DIM)
+        return pltpu.make_async_copy(
+            weight_ref.at[:, pl.ds(first, HEAD_DIM)],
+            held.at[x, :, place * HEAD_DIM : (place + 1) * HEAD_DIM],
+            loads.at[x, place],
+        )
+
+    def store(x):
+        return pltpu.make_async_copy(held.at[x], pack_ref.at[x], stores.at[x])
+
+    for x in range(x_parts):
+        for place in range(places):
+            load(x, place).start()
+
+    def pass_on():
+        for x in range(x_parts):
+            for place in range(places):
+                load(x, place).wait()
+            store(x).start()
 
     @pl.when(jnp.logical_not(picked))
     def _():
         for ref in (cross_ref, own_ref):
             ref[: x_parts * HEAD_DIM, :] = jnp.zeros((x_parts * HEAD_DIM, rows), jnp.bfloat16)
             ref[x_parts * HEAD_DIM :, :] = jnp.full((STAT_ROWS, rows), MASKED, jnp.bfloat16)
-
-    def compute(masked):
+        pass_on()
+
+    def compute(ref, side, masked):
+        first = pl.multiple_of(side * x_parts * HEAD_DIM, HEAD_DIM)
+        heads = q_ref[:, pl.ds(first, x_parts * HEAD_DIM)]
+        scores = lax.dot_general(
+            k_ref[...],
+            jnp.concatenate([heads[:, i * HEAD_DIM : (i + 1) * HEAD_DIM] for i in range(x_parts)], axis=0),
+            (((1,), (1,)), ((), ())),
+            preferred_element_type=jnp.float32,
+        )
+        if masked:
+            position = lax.broadcasted_iota(jnp.int32, scores.shape, 0)
+            scores = jnp.where(position < usable, scores, MASKED)
+        top = jnp.max(scores, axis=0, keepdims=True)
+        expo = jnp.exp2((scores - top) * factor)
+        total = jnp.sum(expo, axis=0, keepdims=True)
+        gathered = jnp.dot(vt_ref[...], expo.astype(jnp.bfloat16), preferred_element_type=jnp.float32)
+        gathered = (gathered / total).astype(jnp.bfloat16)
+        logs = top * factor + jnp.log2(total)
+        for i in range(x_parts):
+            ref[i * HEAD_DIM : (i + 1) * HEAD_DIM, :] = gathered[:, i * rows : (i + 1) * rows]
+        ref[x_parts * HEAD_DIM :, :] = stat_rows([logs[:, i * rows : (i + 1) * rows] for i in range(x_parts)])
+
+    def attend(masked):
+        for copy in fetch:
+            copy.wait()
         vt_ref[...] = v_ref[...].T
-        for ref, side in ((cross_ref, 1 - z), (own_ref, z)):
-            first = pl.multiple_of(side * x_parts * HEAD_DIM, HEAD_DIM)
-            heads = q_ref[:, pl.ds(first, x_parts * HEAD_DIM)]
-            scores = lax.dot_general(
-                k_ref[...],
-                jnp.concatenate([heads[:, i * HEAD_DIM : (i + 1) * HEAD_DIM] for i in range(x_parts)], axis=0),
-                (((1,), (1,)), ((), ())),
-                preferred_element_type=jnp.float32,
-            )
-            if masked:
-                position = lax.broadcasted_iota(jnp.int32, scores.shape, 0)
-                scores = jnp.where(position < usable, scores, MASKED)
-            top = jnp.max(scores, axis=0, keepdims=True)
-            expo = jnp.exp2((scores - top) * factor)
-            total = jnp.sum(expo, axis=0, keepdims=True)
-            gathered = jnp.dot(vt_ref[...], expo.astype(jnp.bfloat16), preferred_element_type=jnp.float32)
-            gathered = (gathered / total).astype(jnp.bfloat16)
-            logs = top * factor + jnp.log2(total)
-            for i in range(x_parts):
-                ref[i * HEAD_DIM : (i + 1) * HEAD_DIM, :] = gathered[:, i * rows : (i + 1) * rows]
-            ref[x_parts * HEAD_DIM :, :] = stat_rows([logs[:, i * rows : (i + 1) * rows] for i in range(x_parts)])
-
-    pl.when(jnp.logical_and(picked, usable >= span))(lambda: compute(False))
-    pl.when(jnp.logical_and(picked, usable < span))(lambda: compute(True))
+        compute(cross_ref, 1 - z, masked)
+        pass_on()
+        compute(own_ref, z, masked)
+
+    pl.when(jnp.logical_and(picked, usable >= span))(lambda: attend(False))
+    pl.when(jnp.logical_and(picked, usable < span))(lambda: attend(True))
+    for x in range(x_parts):
+        store(x).wait()
 
 
 def merged(outs, logs):
@@ -131,17 +145,14 @@
     for head in range(len(own)):
         there = jnp.where(absent, MASKED, other_logs[head])
         out, log = merged([own[head], other[head]], [own_logs[head], there])
-        out = out.astype(jnp.bfloat16)
-        for x in range(out_ref.shape[0]):
-            out_ref[x, head * HEAD_DIM : (head + 1) * HEAD_DIM, :] = out
+        out_ref[head * HEAD_DIM : (head + 1) * HEAD_DIM, :] = out.astype(jnp.bfloat16)
         logs.append(log)
-    stats = stat_rows(logs)
-    for x in range(out_ref.shape[0]):
-        out_ref[x, len(own) * HEAD_DIM :, :] = stats
-
-
-def project_body(parts_ref, kept_ref, given_ref, out_ref):
-    parts = [outs_and_logs(parts_ref[i]) for i in range(parts_ref.shape[0])]
+    out_ref[len(own) * HEAD_DIM :, :] = stat_rows(logs)
+
+
+def project_body(*refs):
+    terms, (kept_ref, given_ref, out_ref) = refs[:-3], refs[-3:]
+    parts = [outs_and_logs(ref[...]) for ref in terms]
     heads = []
     for head in range(len(parts[0][0])):
         out, _ = merged([outs[head] for outs, _ in parts], [logs[head] for _, logs in parts])
@@ -187,28 +198,26 @@
         )
 
     packed = out_weight.shape[1] // x_parts // CORES
-    pack = pl.pallas_call(
-        pack_body,
-        out_shape=shape(x_parts, HEAD_DIM, packed),
-        in_specs=[pl.BlockSpec(memory_space=pl.ANY)],
-        out_specs=pl.BlockSpec(memory_space=pl.ANY),
+    places = packed // HEAD_DIM
+    vmem = pl.BlockSpec(memory_space=pltpu.VMEM)
+    anywhere = pl.BlockSpec(memory_space=pl.ANY)
+    own, cross, pack = pl.pallas_call(
+        attend_body,
+        out_shape=[shape(message, rows)] * 2 + [shape(x_parts, HEAD_DIM, packed)],
+        in_specs=[pl.BlockSpec(memory_space=pltpu.SMEM)] * 2 + [anywhere] * 4,
+        out_specs=[vmem, vmem, anywhere],
         scratch_shapes=[
+            pltpu.VMEM(queries.shape, jnp.bfloat16),
+            pltpu.VMEM(keys.shape, jnp.bfloat16),
+            pltpu.VMEM(values.shape, jnp.bfloat16),
+            pltpu.VMEM((HEAD_DIM, keys.shape[0]), jnp.bfloat16),
             pltpu.VMEM((x_parts, HEAD_DIM, packed), jnp.bfloat16),
-            pltpu.SemaphoreType.DMA((x_parts, packed // HEAD_DIM)),
+            pltpu.SemaphoreType.DMA((3,)),
+            pltpu.SemaphoreType.DMA((x_parts, places)),
             pltpu.SemaphoreType.DMA((x_parts,)),
         ],
-        name="pack",
-    )(out_weight)
-    weight = lax.all_to_all(pack, "x", 0, 0, tiled=True)
-    own, cross = kernel(
-        attend_body,
-        [pl.BlockSpec(memory_space=pltpu.SMEM)] * 2 + whole(3),
-        [shape(message, rows)] * 2,
-        32,
-        scratch_shapes=[
-            pltpu.VMEM((HEAD_DIM, keys.shape[0]), jnp.bfloat16),
-        ],
-    )(lengths, selected, queries, keys, values)
+        name="attend",
+    )(lengths, selected, queries, keys, values, out_weight)
 
     def onward(part, flip):
         pairs = [
@@ -220,10 +229,13 @@
 
     swap = [(s * z_parts + z, s * z_parts + 1 - z) for s in range(segments) for z in range(z_parts) if s % 2 or z == 0]
     other = lax.ppermute(cross, ("segment", "z"), swap)
-    given = lax.ppermute(weight, "segment", [(s, s ^ 1) for s in range(segments)])
-    (terms,) = kernel(merge_body, whole(2), [shape(x_parts, message, rows)], 8)(own, other)
-    terms = lax.all_to_all(terms, "x", 0, 0, tiled=True)
-    (products,) = kernel(project_body, whole(3), [shape(y_parts, z_parts, *tile)], 16)(terms, weight, given)
+    kept = lax.all_to_all(pack, "x", 0, 0, tiled=True)
+    (terms,) = kernel(merge_body, whole(2), [shape(message, rows)], 8)(own, other)
+    shared = [terms]
+    for step in sorted(range(1, x_parts), key=lambda k: -min(k, x_parts - k)):
+        shared.append(lax.ppermute(terms, "x", [(x, (x + step) % x_parts) for x in range(x_parts)]))
+    given = lax.ppermute(kept, "segment", [(s, s ^ 1) for s in range(segments)])
+    (products,) = kernel(project_body, whole(x_parts + 2), [shape(y_parts, z_parts, *tile)], 16)(*shared, kept, given)
     products = lax.all_to_all(products, "head", 0, 0, tiled=True)
     own, cross = kernel(split_sum_body, whole(1), [shape(*tile)] * 2, 8)(products)
 

time: 102 us -> 105 us (1.029)
  the two profiles are of different devices: /device:TPU:1 before, /device:TPU:6 now
where the time goes in v3:
time: 105 us; the launch traced here: 104 us
  blocking collectives  44 us (42%)
  starting transfers between devices  38.4 us (37%)
  waiting for transfers between devices  12.3 us (12%)
  Pallas kernels  8.18 us (8%)
    all_to_all x1, blocking collectives, on_device(): products = lax.all_to_all(products, 'head', 0, 0, tiled=True)  22 us
    all_to_all x1, blocking collectives, on_device(): kept = lax.all_to_all(pack, 'x', 0, 0, tiled=True)  21.9 us
    ppermute x2, starting transfers between devices, onward(): return lax.ppermute(part, ('segment', 'z'), pairs)  18.1 us
    ppermute x3, starting transfers between devices, on_device(): lax.ppermute(terms, 'x', [(x, (x + step) % x_parts) for x in range(x_part...  9.82 us
    ppermute x1, starting transfers between devices, on_device(): other = lax.ppermute(cross, ('segment', 'z'), swap)  8.58 us
    pallas_call x1, Pallas kernels, on_device(): pl.pallas_call(attend_body, out_shape=[shape(message, rows)] * 2 + [shape...  7.44 us
    ppermute x3, waiting for transfers between devices, on_device(): lax.ppermute(terms, 'x', [(x, (x + step) % x_parts) for x in range(x_part...  5.62 us
    ppermute x1, waiting for transfers between devices, on_device(): other = lax.ppermute(cross, ('segment', 'z'), swap)  5.07 us
  transfers between devices with their start and end apart: 7, of which 3 were waited for; matrix products, arithmetic and copies ran while one was open for 0% of the time, Pallas kernels for 0%

profile of v3, /device:TPU:6, one launch (start us, length us, event | category | flops | bytes accessed | tf_op | source)
XLA Modules:
  0.0 104.2 jit_solution(15501783552552311516)
XLA Ops:
  0.7 7.4 %attend.1 = (bf16[528,128]{1,0:T(8,128)(2,1)}, bf16[528,128]{1,0:T(8,128)(2,1)}, bf16[4,128,1024]{2,1,0:T(8,128)(2,1)}) custom-call(s32[1]{0:T(128)S(6)} %copy.7.cached_ref, s32[1,3]{1,0:T(1,128)} %chosen_ref.1, bf16[128,1024]{1,0:T(8,128)(2,1)} %q_hbm.1, bf16[2048,128]{1,0:T(8,128)(2,1)} %k_hbm.1, bf16[2048,128]{1,0:T(8,128)(2,1)} %v_hbm.1, ...), custom_call_target="tpu_custom_call" | custom-call | tf_op jit(solution)/shard_map/attend/pallas_call | solution.py:204
  8.1 0.0 copy-start.1
  8.1 0.0 copy-start
  8.1 21.9 %all_to_all.10.refs_4_ = bf16[4,128,1024]{2,1,0:T(8,128)(2,1)S(1)} all-to-all(bf16[4,128,1024]{2,1,0:T(8,128)(2,1)} %get-tuple-element.12), channel_id=1, replica_groups=mesh['segment'=12,'z'=2,'x'=4,'head'=8] {'x'}, dimensions={0} | all-to-all | bytes 2097152 | tf_op jit(solution)/shard_map/all_to_all | solution.py:232
  30.1 1.9 %collective-permute-start.4 = (bf16[4,128,1024]{2,1,0:T(8,128)(2,1)S(1)}, bf16[4,128,1024]{2,1,0:T(8,128)(2,1)S(1)}, u32[]{:S(2)}, u32[]{:S(2)}) collective-permute-start(bf16[4,128,1024]{2,1,0:T(8,128)(2,1)S(1)} %all_to_all.10.refs_4_), channel_id=1, source_target_pairs={{0,64},{64,0},{128,192},{192,128},{256,320},{320,256},{384,448},{4... | collective-permute-start | bytes 3145736 | tf_op jit(solution)/shard_map/ppermute | solution.py:237
  32.0 0.0 copy-done.1
  32.0 8.6 %collective-permute-start = (bf16[528,128]{1,0:T(8,128)(2,1)S(1)}, bf16[528,128]{1,0:T(8,128)(2,1)S(1)}, u32[]{:S(2)}, u32[]{:S(2)}) collective-permute-start(bf16[528,128]{1,0:T(8,128)(2,1)S(1)} %copy-done.1), channel_id=1, source_target_pairs={{0,32},{64,96},{96,64},{128,160},{192,224},{224,192},{256,288},{32... | collective-permute-start | bytes 405512 | tf_op jit(solution)/shard_map/ppermute | solution.py:231
  40.6 5.1 %collective-permute-done.other_ref = bf16[528,128]{1,0:T(8,128)(2,1)S(1)} collective-permute-done((bf16[528,128]{1,0:T(8,128)(2,1)S(1)}, bf16[528,128]{1,0:T(8,128)(2,1)S(1)}, u32[]{:S(2)}, u32[]{:S(2)}) %collective-permute-start) | collective-permute-done | bytes 135200 | tf_op jit(solution)/shard_map/ppermute | solution.py:231
  45.6 0.1 shard_map.64.refs_0_
  45.7 2.1 %collective-permute-start.3 = (bf16[528,128]{1,0:T(8,128)(2,1)S(1)}, bf16[528,128]{1,0:T(8,128)(2,1)S(1)}, u32[]{:S(2)}, u32[]{:S(2)}) collective-permute-start(bf16[528,128]{1,0:T(8,128)(2,1)S(1)} %shard_map.64.refs_0_), channel_id=1, source_target_pairs={{0,24},{8,0},{16,8},{24,16},{1,25},{9,1},{17,9},{25,17},{2,26},{10... | collective-permute-start | bytes 405512 | tf_op jit(solution)/shard_map/ppermute | solution.py:236
  47.9 4.9 %collective-permute-start.2 = (bf16[528,128]{1,0:T(8,128)(2,1)S(1)}, bf16[528,128]{1,0:T(8,128)(2,1)S(1)}, u32[]{:S(2)}, u32[]{:S(2)}) collective-permute-start(bf16[528,128]{1,0:T(8,128)(2,1)S(1)} %shard_map.64.refs_0_), channel_id=1, source_target_pairs={{0,8},{8,16},{16,24},{24,0},{1,9},{9,17},{17,25},{25,1},{2,10},{10... | collective-permute-start | bytes 405512 | tf_op jit(solution)/shard_map/ppermute | solution.py:236
  52.8 2.8 %collective-permute-start.1 = (bf16[528,128]{1,0:T(8,128)(2,1)S(1)}, bf16[528,128]{1,0:T(8,128)(2,1)S(1)}, u32[]{:S(2)}, u32[]{:S(2)}) collective-permute-start(bf16[528,128]{1,0:T(8,128)(2,1)S(1)} %shard_map.64.refs_0_), channel_id=1, source_target_pairs={{0,16},{8,24},{16,0},{24,8},{1,17},{9,25},{17,1},{25,9},{2,18},{10... | collective-permute-start | bytes 405512 | tf_op jit(solution)/shard_map/ppermute | solution.py:236
  55.6 0.0 collective-permute-done.3.refs_3_
  55.6 0.0 collective-permute-done.2.refs_2_
  55.6 5.6 %collective-permute-done.1.refs_1_ = bf16[528,128]{1,0:T(8,128)(2,1)S(1)} collective-permute-done((bf16[528,128]{1,0:T(8,128)(2,1)S(1)}, bf16[528,128]{1,0:T(8,128)(2,1)S(1)}, u32[]{:S(2)}, u32[]{:S(2)}) %collective-permute-start.1) | collective-permute-done | bytes 135200 | tf_op jit(solution)/shard_map/ppermute | solution.py:236
  61.2 0.0 collective-permute-done.4.refs_5_
  61.2 0.6 shard_map.65
  61.8 22.0 %all_to_all.11.parts_ref = bf16[8,2,128,128]{3,2,1,0:T(8,128)(2,1)S(1)} all-to-all(bf16[8,2,128,128]{3,2,1,0:T(8,128)(2,1)S(1)} %shard_map.65), channel_id=1, replica_groups=mesh['segment'=12,'z'=2,'x'=4,'head'=8] {'head'}, dimensions={0} | all-to-all | bytes 1048576 | tf_op jit(solution)/shard_map/all_to_all | solution.py:239
  83.9 0.1 shard_map.66
  83.9 1.9 %collective-permute-start.5 = (bf16[128,128]{1,0:T(8,128)(2,1)S(1)}, bf16[128,128]{1,0:T(8,128)(2,1)S(1)}, u32[]{:S(2)}, u32[]{:S(2)}) collective-permute-start(bf16[128,128]{1,0:T(8,128)(2,1)S(1)} %get-tuple-element.13), channel_id=1, source_target_pairs={{0,64},{32,96},{64,128},{96,160},{128,192},{160,224},{192,256},{22... | collective-permute-start | bytes 98312 | tf_op jit(solution)/shard_map/ppermute | solution.py:228
  85.9 16.2 %collective-permute-start.6 = (bf16[128,128]{1,0:T(8,128)(2,1)S(1)}, bf16[128,128]{1,0:T(8,128)(2,1)S(1)}, u32[]{:S(2)}, u32[]{:S(2)}) collective-permute-start(bf16[128,128]{1,0:T(8,128)(2,1)S(1)} %get-tuple-element.14), channel_id=1, source_target_pairs={{0,96},{32,64},{64,160},{96,128},{128,224},{160,192},{192,288},{22... | collective-permute-start | bytes 98312 | tf_op jit(solution)/shard_map/ppermute | solution.py:228
  102.0 0.0 collective-permute-done.5
  102.0 1.6 %collective-permute-done.6 = bf16[128,128]{1,0:T(8,128)(2,1)S(1)} collective-permute-done((bf16[128,128]{1,0:T(8,128)(2,1)S(1)}, bf16[128,128]{1,0:T(8,128)(2,1)S(1)}, u32[]{:S(2)}, u32[]{:S(2)}) %collective-permute-start.6) | collective-permute-done | bytes 32800 | tf_op jit(solution)/shard_map/ppermute | solution.py:228
  103.6 0.6 add_convert_fusion
  (1 shorter events, 0.0 us)
Async XLA Ops:
  8.1 23.9 %copy-start.1 = (bf16[528,128]{1,0:T(8,128)(2,1)S(1)}, bf16[528,128]{1,0:T(8,128)(2,1)}, u32[]{:S(2)}) copy-start(bf16[528,128]{1,0:T(8,128)(2,1)} %get-tuple-element.11) | copy-start | bytes 405508
  8.1 37.5 %copy-start = (bf16[528,128]{1,0:T(8,128)(2,1)S(1)}, bf16[528,128]{1,0:T(8,128)(2,1)}, u32[]{:S(2)}) copy-start(bf16[528,128]{1,0:T(8,128)(2,1)} %get-tuple-element.10.own_ref) | copy-start | bytes 405508
  30.1 31.2 %collective-permute-start.4 = (bf16[4,128,1024]{2,1,0:T(8,128)(2,1)S(1)}, bf16[4,128,1024]{2,1,0:T(8,128)(2,1)S(1)}, u32[]{:S(2)}, u32[]{:S(2)}) collective-permute-start(bf16[4,128,1024]{2,1,0:T(8,128)(2,1)S(1)} %all_to_all.10.refs_4_), channel_id=1, source_target_pairs={{0,64},{64,0},{128,192},{192,128},{256,320},{320,256},{384,448},{4... | collective-permute-start | bytes 3145736 | tf_op jit(solution)/shard_map/ppermute | solution.py:237
  32.0 13.7 %collective-permute-start = (bf16[528,128]{1,0:T(8,128)(2,1)S(1)}, bf16[528,128]{1,0:T(8,128)(2,1)S(1)}, u32[]{:S(2)}, u32[]{:S(2)}) collective-permute-start(bf16[528,128]{1,0:T(8,128)(2,1)S(1)} %copy-done.1), channel_id=1, source_target_pairs={{0,32},{64,96},{96,64},{128,160},{192,224},{224,192},{256,288},{32... | collective-permute-start | bytes 405512 | tf_op jit(solution)/shard_map/ppermute | solution.py:231
  45.7 9.8 %collective-permute-start.3 = (bf16[528,128]{1,0:T(8,128)(2,1)S(1)}, bf16[528,128]{1,0:T(8,128)(2,1)S(1)}, u32[]{:S(2)}, u32[]{:S(2)}) collective-permute-start(bf16[528,128]{1,0:T(8,128)(2,1)S(1)} %shard_map.64.refs_0_), channel_id=1, source_target_pairs={{0,24},{8,0},{16,8},{24,16},{1,25},{9,1},{17,9},{25,17},{2,26},{10... | collective-permute-start | bytes 405512 | tf_op jit(solution)/shard_map/ppermute | solution.py:236
  47.9 7.7 %collective-permute-start.2 = (bf16[528,128]{1,0:T(8,128)(2,1)S(1)}, bf16[528,128]{1,0:T(8,128)(2,1)S(1)}, u32[]{:S(2)}, u32[]{:S(2)}) collective-permute-start(bf16[528,128]{1,0:T(8,128)(2,1)S(1)} %shard_map.64.refs_0_), channel_id=1, source_target_pairs={{0,8},{8,16},{16,24},{24,0},{1,9},{9,17},{17,25},{25,1},{2,10},{10... | collective-permute-start | bytes 405512 | tf_op jit(solution)/shard_map/ppermute | solution.py:236
  52.8 8.4 %collective-permute-start.1 = (bf16[528,128]{1,0:T(8,128)(2,1)S(1)}, bf16[528,128]{1,0:T(8,128)(2,1)S(1)}, u32[]{:S(2)}, u32[]{:S(2)}) collective-permute-start(bf16[528,128]{1,0:T(8,128)(2,1)S(1)} %shard_map.64.refs_0_), channel_id=1, source_target_pairs={{0,16},{8,24},{16,0},{24,8},{1,17},{9,25},{17,1},{25,9},{2,18},{10... | collective-permute-start | bytes 405512 | tf_op jit(solution)/shard_map/ppermute | solution.py:236
  83.9 18.1 %collective-permute-start.5 = (bf16[128,128]{1,0:T(8,128)(2,1)S(1)}, bf16[128,128]{1,0:T(8,128)(2,1)S(1)}, u32[]{:S(2)}, u32[]{:S(2)}) collective-permute-start(bf16[128,128]{1,0:T(8,128)(2,1)S(1)} %get-tuple-element.13), channel_id=1, source_target_pairs={{0,64},{32,96},{64,128},{96,160},{128,192},{160,224},{192,256},{22... | collective-permute-start | bytes 98312 | tf_op jit(solution)/shard_map/ppermute | solution.py:228
  85.9 17.8 %collective-permute-start.6 = (bf16[128,128]{1,0:T(8,128)(2,1)S(1)}, bf16[128,128]{1,0:T(8,128)(2,1)S(1)}, u32[]{:S(2)}, u32[]{:S(2)}) collective-permute-start(bf16[128,128]{1,0:T(8,128)(2,1)S(1)} %get-tuple-element.14), channel_id=1, source_target_pairs={{0,96},{32,64},{64,160},{96,128},{128,224},{160,192},{192,288},{22... | collective-permute-start | bytes 98312 | tf_op jit(solution)/shard_map/ppermute | solution.py:228

commit v4 on v3

--- a/solution.py
+++ b/solution.py
@@ -41,8 +41,35 @@
     return outs, [stats[3 * i : 3 * i + 1] + stats[3 * i + 1 : 3 * i + 2] + stats[3 * i + 2 : 3 * i + 3] for i in range(count)]
 
 
-def attend_body(cached_ref, chosen_ref, q_hbm, k_hbm, v_hbm, weight_ref, own_ref, cross_ref, pack_ref, *scratch):
-    q_ref, k_ref, v_ref, vt_ref, held, fetches, loads, stores = scratch
+def pack_body(weight_ref, out_ref, held, loads, stores):
+    x_parts = out_ref.shape[0]
+    places = out_ref.shape[2] // HEAD_DIM
+    core = lax.axis_index("segment") % CORES
+
+    def load(x, place):
+        first = pl.multiple_of(((core * places + place) * x_parts + x) * HEAD_DIM, HEAD_DIM)
+        return pltpu.make_async_copy(
+            weight_ref.at[:, pl.ds(first, HEAD_DIM)],
+            held.at[x, :, place * HEAD_DIM : (place + 1) * HEAD_DIM],
+            loads.at[x, place],
+        )
+
+    def store(x):
+        return pltpu.make_async_copy(held.at[x], out_ref.at[x], stores.at[x])
+
+    for x in range(x_parts):
+        for place in range(places):
+            load(x, place).start()
+    for x in range(x_parts):
+        for place in range(places):
+            load(x, place).wait()
+        store(x).start()
+    for x in range(x_parts):
+        store(x).wait()
+
+
+def attend_body(cached_ref, chosen_ref, q_hbm, k_hbm, v_hbm, own_ref, cross_ref, *scratch):
+    q_ref, k_ref, v_ref, vt_ref, fetches = scratch
     x_parts = own_ref.shape[0] // HEAD_DIM
     rows = q_ref.shape[0]
     span = k_ref.shape[0]
@@ -62,36 +89,11 @@
         for copy in fetch:
             copy.start()
 
-    places = pack_ref.shape[2] // HEAD_DIM
-    core = lax.axis_index("segment") % CORES
-
-    def load(x, place):
-        first = pl.multiple_of(((core * places + place) * x_parts + x) * HEAD_DIM, HEAD_DIM)
-        return pltpu.make_async_copy(
-            weight_ref.at[:, pl.ds(first, HEAD_DIM)],
-            held.at[x, :, place * HEAD_DIM : (place + 1) * HEAD_DIM],
-            loads.at[x, place],
-        )
-
-    def store(x):
-        return pltpu.make_async_copy(held.at[x], pack_ref.at[x], stores.at[x])
-
-    for x in range(x_parts):
-        for place in range(places):
-            load(x, place).start()
-
-    def pass_on():
-        for x in range(x_parts):
-            for place in range(places):
-                load(x, place).wait()
-            store(x).start()
-
     @pl.when(jnp.logical_not(picked))
     def _():
         for ref in (cross_ref, own_ref):
             ref[: x_parts * HEAD_DIM, :] = jnp.zeros((x_parts * HEAD_DIM, rows), jnp.bfloat16)
             ref[x_parts * HEAD_DIM :, :] = jnp.full((STAT_ROWS, rows), MASKED, jnp.bfloat16)
-        pass_on()
 
     def compute(ref, side, masked):
         first = pl.multiple_of(side * x_parts * HEAD_DIM, HEAD_DIM)
@@ -120,13 +122,10 @@
             copy.wait()
         vt_ref[...] = v_ref[...].T
         compute(cross_ref, 1 - z, masked)
-        pass_on()
         compute(own_ref, z, masked)
 
     pl.when(jnp.logical_and(picked, usable >= span))(lambda: attend(False))
     pl.when(jnp.logical_and(picked, usable < span))(lambda: attend(True))
-    for x in range(x_parts):
-        store(x).wait()
 
 
 def merged(outs, logs):
@@ -201,23 +200,32 @@
     places = packed // HEAD_DIM
     vmem = pl.BlockSpec(memory_space=pltpu.VMEM)
     anywhere = pl.BlockSpec(memory_space=pl.ANY)
-    own, cross, pack = pl.pallas_call(
+    own, cross = pl.pallas_call(
         attend_body,
-        out_shape=[shape(message, rows)] * 2 + [shape(x_parts, HEAD_DIM, packed)],
-        in_specs=[pl.BlockSpec(memory_space=pltpu.SMEM)] * 2 + [anywhere] * 4,
-        out_specs=[vmem, vmem, anywhere],
+        out_shape=[shape(message, rows)] * 2,
+        in_specs=[pl.BlockSpec(memory_space=pltpu.SMEM)] * 2 + [anywhere] * 3,
+        out_specs=[vmem] * 2,
         scratch_shapes=[
             pltpu.VMEM(queries.shape, jnp.bfloat16),
             pltpu.VMEM(keys.shape, jnp.bfloat16),
             pltpu.VMEM(values.shape, jnp.bfloat16),
             pltpu.VMEM((HEAD_DIM, keys.shape[0]), jnp.bfloat16),
+            pltpu.SemaphoreType.DMA((3,)),
+        ],
+        name="attend",
+    )(lengths, selected, queries, keys, values)
+    pack = pl.pallas_call(
+        pack_body,
+        out_shape=shape(x_parts, HEAD_DIM, packed),
+        in_specs=[anywhere],
+        out_specs=anywhere,
+        scratch_shapes=[
             pltpu.VMEM((x_parts, HEAD_DIM, packed), jnp.bfloat16),
-            pltpu.SemaphoreType.DMA((3,)),
             pltpu.SemaphoreType.DMA((x_parts, places)),
             pltpu.SemaphoreType.DMA((x_parts,)),
         ],
-        name="attend",
-    )(lengths, selected, queries, keys, values, out_weight)
+        name="pack",
+    )(out_weight)
 
     def onward(part, flip):
         pairs = [

time: 105 us -> 105 us (level)
  the two profiles are of different devices: /device:TPU:6 before, /device:TPU:1 now
where the time goes in v4:
time: 105 us
  starting transfers between devices  42 us (40%)
  blocking collectives  39.2 us (37%)
  waiting for transfers between devices  12.2 us (12%)
  Pallas kernels  9.1 us (9%)
    all_to_all x1, blocking collectives, on_device(): products = lax.all_to_all(products, 'head', 0, 0, tiled=True)  24.7 us
    all_to_all x1, blocking collectives, on_device(): kept = lax.all_to_all(pack, 'x', 0, 0, tiled=True)  14.6 us
    ppermute x2, starting transfers between devices, onward(): return lax.ppermute(part, ('segment', 'z'), pairs)  14.5 us
    ppermute x1, starting transfers between devices, on_device(): given = lax.ppermute(kept, 'segment', [(s, s ^ 1) for s in range(segments)])  12.2 us
    ppermute x3, starting transfers between devices, on_device(): lax.ppermute(terms, 'x', [(x, (x + step) % x_parts) for x in range(x_part...  9.14 us
    ppermute x1, waiting for transfers between devices, on_device(): other = lax.ppermute(cross, ('segment', 'z'), swap)  6.23 us
    ppermute x1, starting transfers between devices, on_device(): other = lax.ppermute(cross, ('segment', 'z'), swap)  6.2 us
    pallas_call x1, Pallas kernels, on_device(): pl.pallas_call(attend_body, out_shape=[shape(message, rows)] * 2, in_spec...  6.16 us
  transfers between devices with their start and end apart: 7, of which 3 were waited for; matrix products, arithmetic and copies ran while one was open for 0% of the time, Pallas kernels for 6%

profile of v4, /device:TPU:1, one launch (start us, length us, event | category | flops | bytes accessed | tf_op | source)
XLA Modules:
  0.0 104.9 jit_solution(12876434747946632727)
XLA Ops:
  0.0 2.2 %pack.1 = bf16[4,128,1024]{2,1,0:T(8,128)(2,1)} custom-call(bf16[128,8192]{1,0:T(8,128)(2,1)} %weight_ref.1), custom_call_target="tpu_custom_call" | custom-call | tf_op jit(solution)/shard_map/pack/pallas_call | solution.py:217
  2.2 14.6 %all_to_all.10.refs_4_ = bf16[4,128,1024]{2,1,0:T(8,128)(2,1)S(1)} all-to-all(bf16[4,128,1024]{2,1,0:T(8,128)(2,1)} %pack.1), channel_id=1, replica_groups=mesh['segment'=12,'z'=2,'x'=4,'head'=8] {'x'}, dimensions={0} | all-to-all | bytes 2097152 | tf_op jit(solution)/shard_map/all_to_all | solution.py:240
  16.8 12.2 %collective-permute-start.4 = (bf16[4,128,1024]{2,1,0:T(8,128)(2,1)S(1)}, bf16[4,128,1024]{2,1,0:T(8,128)(2,1)S(1)}, u32[]{:S(2)}, u32[]{:S(2)}) collective-permute-start(bf16[4,128,1024]{2,1,0:T(8,128)(2,1)S(1)} %all_to_all.10.refs_4_), channel_id=1, source_target_pairs={{0,64},{64,0},{128,192},{192,128},{256,320},{320,256},{384,448},{4... | collective-permute-start | bytes 3145736 | tf_op jit(solution)/shard_map/ppermute | solution.py:245
  29.6 6.2 %attend.1 = (bf16[528,128]{1,0:T(8,128)(2,1)}, bf16[528,128]{1,0:T(8,128)(2,1)}) custom-call(s32[1]{0:T(128)S(6)} %copy.7.cached_ref, s32[1,3]{1,0:T(1,128)} %chosen_ref.1, bf16[128,1024]{1,0:T(8,128)(2,1)} %q_hbm.1, bf16[2048,128]{1,0:T(8,128)(2,1)} %k_hbm.1, bf16[2048,128]{1,0:T(8,128)(2,1)} %v_hbm.1), custom_call_target="tpu_custom_call" | custom-call | tf_op jit(solution)/shard_map/attend/pallas_call | solution.py:203
  35.8 6.2 %collective-permute-start = (bf16[528,128]{1,0:T(8,128)(2,1)}, bf16[528,128]{1,0:T(8,128)(2,1)S(1)}, u32[]{:S(2)}, u32[]{:S(2)}) collective-permute-start(bf16[528,128]{1,0:T(8,128)(2,1)} %get-tuple-element.10), channel_id=1, source_target_pairs={{0,32},{64,96},{96,64},{128,160},{192,224},{224,192},{256,288},{32... | collective-permute-start | bytes 405512 | tf_op jit(solution)/shard_map/ppermute | solution.py:239
  42.0 6.2 %collective-permute-done.other_ref = bf16[528,128]{1,0:T(8,128)(2,1)S(1)} collective-permute-done((bf16[528,128]{1,0:T(8,128)(2,1)}, bf16[528,128]{1,0:T(8,128)(2,1)S(1)}, u32[]{:S(2)}, u32[]{:S(2)}) %collective-permute-start) | collective-permute-done | bytes 135200 | tf_op jit(solution)/shard_map/ppermute | solution.py:239
  48.2 0.0 copy-start
  48.2 0.9 copy-done
  49.1 0.1 shard_map.64.refs_0_
  49.2 4.1 %collective-permute-start.3 = (bf16[528,128]{1,0:T(8,128)(2,1)S(1)}, bf16[528,128]{1,0:T(8,128)(2,1)S(1)}, u32[]{:S(2)}, u32[]{:S(2)}) collective-permute-start(bf16[528,128]{1,0:T(8,128)(2,1)S(1)} %shard_map.64.refs_0_), channel_id=1, source_target_pairs={{0,24},{8,0},{16,8},{24,16},{1,25},{9,1},{17,9},{25,17},{2,26},{10... | collective-permute-start | bytes 405512 | tf_op jit(solution)/shard_map/ppermute | solution.py:244
  53.4 1.9 %collective-permute-start.2 = (bf16[528,128]{1,0:T(8,128)(2,1)S(1)}, bf16[528,128]{1,0:T(8,128)(2,1)S(1)}, u32[]{:S(2)}, u32[]{:S(2)}) collective-permute-start(bf16[528,128]{1,0:T(8,128)(2,1)S(1)} %shard_map.64.refs_0_), channel_id=1, source_target_pairs={{0,8},{8,16},{16,24},{24,0},{1,9},{9,17},{17,25},{25,1},{2,10},{10... | collective-permute-start | bytes 405512 | tf_op jit(solution)/shard_map/ppermute | solution.py:244
  55.3 3.1 %collective-permute-start.1 = (bf16[528,128]{1,0:T(8,128)(2,1)S(1)}, bf16[528,128]{1,0:T(8,128)(2,1)S(1)}, u32[]{:S(2)}, u32[]{:S(2)}) collective-permute-start(bf16[528,128]{1,0:T(8,128)(2,1)S(1)} %shard_map.64.refs_0_), channel_id=1, source_target_pairs={{0,16},{8,24},{16,0},{24,8},{1,17},{9,25},{17,1},{25,9},{2,18},{10... | collective-permute-start | bytes 405512 | tf_op jit(solution)/shard_map/ppermute | solution.py:244
  58.4 0.0 collective-permute-done.3.refs_3_
  58.4 4.8 %collective-permute-done.2.refs_2_ = bf16[528,128]{1,0:T(8,128)(2,1)S(1)} collective-permute-done((bf16[528,128]{1,0:T(8,128)(2,1)S(1)}, bf16[528,128]{1,0:T(8,128)(2,1)S(1)}, u32[]{:S(2)}, u32[]{:S(2)}) %collective-permute-start.2) | collective-permute-done | bytes 135200 | tf_op jit(solution)/shard_map/ppermute | solution.py:244
  63.2 0.0 collective-permute-done.1.refs_1_
  63.2 0.0 collective-permute-done.4.refs_5_
  63.2 0.6 shard_map.65
  63.8 24.7 %all_to_all.11.parts_ref = bf16[8,2,128,128]{3,2,1,0:T(8,128)(2,1)S(1)} all-to-all(bf16[8,2,128,128]{3,2,1,0:T(8,128)(2,1)S(1)} %shard_map.65), channel_id=1, replica_groups=mesh['segment'=12,'z'=2,'x'=4,'head'=8] {'head'}, dimensions={0} | all-to-all | bytes 1048576 | tf_op jit(solution)/shard_map/all_to_all | solution.py:247
  88.5 0.1 shard_map.66
  88.6 3.7 %collective-permute-start.5 = (bf16[128,128]{1,0:T(8,128)(2,1)S(1)}, bf16[128,128]{1,0:T(8,128)(2,1)S(1)}, u32[]{:S(2)}, u32[]{:S(2)}) collective-permute-start(bf16[128,128]{1,0:T(8,128)(2,1)S(1)} %get-tuple-element.11), channel_id=1, source_target_pairs={{0,64},{32,96},{64,128},{96,160},{128,192},{160,224},{192,256},{22... | collective-permute-start | bytes 98312 | tf_op jit(solution)/shard_map/ppermute | solution.py:236
  92.3 10.8 %collective-permute-start.6 = (bf16[128,128]{1,0:T(8,128)(2,1)S(1)}, bf16[128,128]{1,0:T(8,128)(2,1)S(1)}, u32[]{:S(2)}, u32[]{:S(2)}) collective-permute-start(bf16[128,128]{1,0:T(8,128)(2,1)S(1)} %get-tuple-element.12), channel_id=1, source_target_pairs={{0,96},{32,64},{64,160},{96,128},{128,224},{160,192},{192,288},{22... | collective-permute-start | bytes 98312 | tf_op jit(solution)/shard_map/ppermute | solution.py:236
  103.1 0.0 collective-permute-done.5
  103.1 1.2 %collective-permute-done.6 = bf16[128,128]{1,0:T(8,128)(2,1)S(1)} collective-permute-done((bf16[128,128]{1,0:T(8,128)(2,1)S(1)}, bf16[128,128]{1,0:T(8,128)(2,1)S(1)}, u32[]{:S(2)}, u32[]{:S(2)}) %collective-permute-start.6) | collective-permute-done | bytes 32800 | tf_op jit(solution)/shard_map/ppermute | solution.py:236
  104.2 0.6 add_convert_fusion
Async XLA Ops:
  16.8 46.4 %collective-permute-start.4 = (bf16[4,128,1024]{2,1,0:T(8,128)(2,1)S(1)}, bf16[4,128,1024]{2,1,0:T(8,128)(2,1)S(1)}, u32[]{:S(2)}, u32[]{:S(2)}) collective-permute-start(bf16[4,128,1024]{2,1,0:T(8,128)(2,1)S(1)} %all_to_all.10.refs_4_), channel_id=1, source_target_pairs={{0,64},{64,0},{128,192},{192,128},{256,320},{320,256},{384,448},{4... | collective-permute-start | bytes 3145736 | tf_op jit(solution)/shard_map/ppermute | solution.py:245
  35.8 12.4 %collective-permute-start = (bf16[528,128]{1,0:T(8,128)(2,1)}, bf16[528,128]{1,0:T(8,128)(2,1)S(1)}, u32[]{:S(2)}, u32[]{:S(2)}) collective-permute-start(bf16[528,128]{1,0:T(8,128)(2,1)} %get-tuple-element.10), channel_id=1, source_target_pairs={{0,32},{64,96},{96,64},{128,160},{192,224},{224,192},{256,288},{32... | collective-permute-start | bytes 405512 | tf_op jit(solution)/shard_map/ppermute | solution.py:239
  48.2 0.9 copy-start
  49.2 9.2 %collective-permute-start.3 = (bf16[528,128]{1,0:T(8,128)(2,1)S(1)}, bf16[528,128]{1,0:T(8,128)(2,1)S(1)}, u32[]{:S(2)}, u32[]{:S(2)}) collective-permute-start(bf16[528,128]{1,0:T(8,128)(2,1)S(1)} %shard_map.64.refs_0_), channel_id=1, source_target_pairs={{0,24},{8,0},{16,8},{24,16},{1,25},{9,1},{17,9},{25,17},{2,26},{10... | collective-permute-start | bytes 405512 | tf_op jit(solution)/shard_map/ppermute | solution.py:244
  53.4 9.9 %collective-permute-start.2 = (bf16[528,128]{1,0:T(8,128)(2,1)S(1)}, bf16[528,128]{1,0:T(8,128)(2,1)S(1)}, u32[]{:S(2)}, u32[]{:S(2)}) collective-permute-start(bf16[528,128]{1,0:T(8,128)(2,1)S(1)} %shard_map.64.refs_0_), channel_id=1, source_target_pairs={{0,8},{8,16},{16,24},{24,0},{1,9},{9,17},{17,25},{25,1},{2,10},{10... | collective-permute-start | bytes 405512 | tf_op jit(solution)/shard_map/ppermute | solution.py:244
  55.3 7.9 %collective-permute-start.1 = (bf16[528,128]{1,0:T(8,128)(2,1)S(1)}, bf16[528,128]{1,0:T(8,128)(2,1)S(1)}, u32[]{:S(2)}, u32[]{:S(2)}) collective-permute-start(bf16[528,128]{1,0:T(8,128)(2,1)S(1)} %shard_map.64.refs_0_), channel_id=1, source_target_pairs={{0,16},{8,24},{16,0},{24,8},{1,17},{9,25},{17,1},{25,9},{2,18},{10... | collective-permute-start | bytes 405512 | tf_op jit(solution)/shard_map/ppermute | solution.py:244
  88.6 14.5 %collective-permute-start.5 = (bf16[128,128]{1,0:T(8,128)(2,1)S(1)}, bf16[128,128]{1,0:T(8,128)(2,1)S(1)}, u32[]{:S(2)}, u32[]{:S(2)}) collective-permute-start(bf16[128,128]{1,0:T(8,128)(2,1)S(1)} %get-tuple-element.11), channel_id=1, source_target_pairs={{0,64},{32,96},{64,128},{96,160},{128,192},{160,224},{192,256},{22... | collective-permute-start | bytes 98312 | tf_op jit(solution)/shard_map/ppermute | solution.py:236
  92.3 11.9 %collective-permute-start.6 = (bf16[128,128]{1,0:T(8,128)(2,1)S(1)}, bf16[128,128]{1,0:T(8,128)(2,1)S(1)}, u32[]{:S(2)}, u32[]{:S(2)}) collective-permute-start(bf16[128,128]{1,0:T(8,128)(2,1)S(1)} %get-tuple-element.12), channel_id=1, source_target_pairs={{0,96},{32,64},{64,160},{96,128},{128,224},{160,192},{192,288},{22... | collective-permute-start | bytes 98312 | tf_op jit(solution)/shard_map/ppermute | solution.py:236
